TPU v7x, 32 devices: a whole 2x2x4 slice. The times are simulated.
32 devices in a mesh: cfg: 2 (over x), sx: 16 (over z, y, core).
Axes of the slice: x: 2, y: 2, z: 4, core: 2. Of those that a mesh axis runs over, the one named last changes fastest.
Arguments:
- eigvecs: bfloat16 [512, 2, 3, 16, 1024], P('cfg', None, None, 'sx'), parts along dimension 0, may hold values from -6 to 6
- link_seed: int32 [6], P('cfg'), parts along dimension 0, may hold values from 1 to 46336
- ownership: int32 [2080], replicated, may hold values from 0 to 2079, each once
Outputs:
- elementals: float32 [4160, 96], P(('cfg', 'sx')), parts along dimension 0
There are 2 independent parts, one for each index of `cfg`. A program takes and returns all parts, laid end to end along the dimension named above; an argument that names none is the same for every part. Nothing has to cross between parts.
Inputs may be any that keep to these rules, and one draw needn't show every extreme that they name: ownership is a permutation of the pair tiles 0 to 2079.
All inputs are finite; a program needn't handle non-finite values.
Results may differ from a plain program's by a relative error of at most 0.0029.
Values may be sent and summed in bfloat16 or wider, within the bound.
A program may use at most 192 MiB of HBM per device.

v0:
```python
import functools
import math

import jax
import jax.numpy as jnp
from jax import lax
from jax.experimental import pallas as pl
from jax.experimental.pallas import tpu as pltpu
from jax.sharding import PartitionSpec as P

TM = 4
NZ = 64
MODULUS = 46337
LANES = 128
ROWS = 16
PARTS = 2
LARGE = 32 * 1024 * 1024
SMALL = 8 * 1024 * 1024
MESH = pl.DeviceIdType.MESH
F32 = jnp.float32
BF16 = jnp.bfloat16


def from_behind(block, axis, distance):
    devices = range(lax.axis_size(axis))
    route = [((i - distance) % len(devices), i) for i in devices]
    return lax.ppermute(block, axis, route)


def quotient(value):
    q = jnp.floor(value.astype(F32) * (1.0 / MODULUS)).astype(jnp.int32)
    rest = value - q * MODULUS
    q = jnp.where(rest < 0, q - 1, jnp.where(rest >= MODULUS, q + 1, q))
    return q


def modulo(value):
    return value - quotient(value) * MODULUS


def links(seed, first_site, shape):
    code = (
        first_site
        + lax.broadcasted_iota(jnp.int32, shape, 0) * LANES
        + lax.broadcasted_iota(jnp.int32, shape, 1)
    )
    high = quotient(code)
    low = code - high * MODULUS
    mixed = modulo(seed * seed + low)
    mixed = modulo(mixed * mixed + high * 977 + 31)
    th = []
    for k in range(7):
        g = modulo(mixed + (5171 * k + 1))
        g = modulo(g * g + low)
        g = modulo(g * g + 12345)
        th.append(g.astype(F32) * (2.0 * math.pi / MODULUS) - math.pi)
    ca, sa = jnp.cos(th[0]), jnp.sin(th[0])
    cb, sb = jnp.cos(th[1]), jnp.sin(th[1])
    cg, sg = jnp.cos(th[2]), jnp.sin(th[2])
    rot = [
        [ca * cb * cg - sa * sg, -ca * cb * sg - sa * cg, ca * sb],
        [sa * cb * cg + ca * sg, -sa * cb * sg + ca * cg, sa * sb],
        [-sb * cg, sb * sg, cb],
    ]
    left = [th[3], th[4], -th[3] - th[4]]
    right = [th[5], th[6], -th[5] - th[6]]
    real, imag = [], []
    for r in range(3):
        for c in range(3):
            angle = left[r] + right[c]
            real.append(rot[r][c] * jnp.cos(angle))
            imag.append(rot[r][c] * jnp.sin(angle))
    return real + imag


def shift_plane(v_refs, sv_ref, kind):
    wide = 2 * LANES
    part, sites = v_refs[0].shape[1], v_refs[0].shape[2]
    row = lax.broadcasted_iota(jnp.int32, (wide, wide), 0)
    col = lax.broadcasted_iota(jnp.int32, (wide, wide), 1)
    if kind == 1:
        source = col + NZ
    else:
        source = jnp.where(col % NZ == NZ - 1, col - (NZ - 1), col + 1)
    move = (row == source).astype(F32).astype(BF16)
    carry_in = (row + wide == source).astype(F32).astype(BF16)[:LANES]
    for j, v_ref in enumerate(v_refs):
        rows = slice(j * part, (j + 1) * part)

        def component(q, carry, v_ref=v_ref, rows=rows):
            for at in range(0, sites, wide):
                x = jnp.dot(v_ref[q, :, at : at + wide], move, preferred_element_type=F32)
                if kind == 1:
                    after = (at + wide) % sites
                    x = x + jnp.dot(
                        v_ref[q, :, after : after + LANES],
                        carry_in,
                        preferred_element_type=F32,
                    )
                sv_ref[q, rows, at : at + wide] = x.astype(BF16)
            return carry

        lax.fori_loop(0, 6, component, 0)


def fill_hops(u_ref, d, src_ref, h_ref):
    modes, sites = src_ref.shape[1], src_ref.shape[2]

    def chunk_step(k, carry):
        u = [
            jnp.broadcast_to(u_ref[d, e, pl.ds(k, 1), :], (8, LANES)) for e in range(18)
        ]
        at = pl.ds(pl.multiple_of(k * LANES, LANES), LANES)

        def rows_step(g, carry):
            rows = pl.ds(pl.multiple_of(g * ROWS, ROWS), ROWS)
            vec = [src_ref[q, rows, at].astype(F32) for q in range(6)]
            parts = []
            for lo in (0, 8):
                v = [x[lo : lo + 8] for x in vec]
                out = []
                for c in range(3):
                    re = im = None
                    for s in range(3):
                        ur, ui = u[3 * c + s], u[9 + 3 * c + s]
                        a = ur * v[s] - ui * v[3 + s]
                        b = ur * v[3 + s] + ui * v[s]
                        re = a if re is None else re + a
                        im = b if im is None else im + b
                    out.append((re, im))
                parts.append(out)
            for c in range(3):
                for t in range(2):
                    both = jnp.concatenate([parts[0][c][t], parts[1][c][t]], 0)
                    h_ref[3 * t + c, rows, at] = both.astype(BF16)
            return carry

        return lax.fori_loop(0, modes // ROWS, rows_step, carry, unroll=2)

    lax.fori_loop(0, sites // LANES, chunk_step, 0)


def negate_imag(v_refs, nv_ref):
    part = v_refs[0].shape[1]
    for j, v_ref in enumerate(v_refs):
        for c in range(3):
            nv_ref[c, j * part : (j + 1) * part] = -v_ref[3 + c]


def gram(v_refs, nv_ref, h_ref):
    total = None
    for q in range(6):
        if q < 3:
            tail = [nv_ref[q]]
        else:
            tail = [r[q - 3] for r in v_refs]
        left = jnp.concatenate([r[q] for r in v_refs] + tail, 0)
        term = lax.dot_general(
            left, h_ref[q], (((1,), (1,)), ((), ())), preferred_element_type=F32
        )
        total = term if total is None else total + term
    return total


def pack_products(total, w_ref, base):
    modes = total.shape[0] // 2
    half = modes // 2
    re, im = total[:modes], total[modes:]
    row = lax.broadcasted_iota(jnp.int32, (half, half), 0)
    col = lax.broadcasted_iota(jnp.int32, (half, half), 1)
    re_top = re[:half, :half] - re[:half, :half].T
    re_low = re[half:, half:] - re[half:, half:].T
    im_top = im[:half, :half] + im[:half, :half].T
    im_low = im[half:, half:] + im[half:, half:].T
    re_mix = jnp.where(row < col, re_top, re_low)
    w_ref[base] = jnp.where(row == col, im_low, re_mix)
    w_ref[base + 1] = re[:half, half:] - re[half:, :half].T
    w_ref[base + 2] = jnp.where(row <= col, im_top, im_low)
    w_ref[base + 3] = im[:half, half:] + im[half:, :half].T


def yz_kernel(seed_ref, *refs):
    v_refs, (w_ref, ux_ref, u_ref, sv_ref, h_ref, nv_ref) = refs[:-6], refs[-6:]
    sites = v_refs[0].shape[2]
    shape = (sites // LANES, LANES)
    first = lax.axis_index("sx") * sites
    for d in (1, 2, 0):
        for e, entry in enumerate(links(seed_ref[d], first, shape)):
            if d == 0:
                ux_ref[0, e] = entry
            else:
                u_ref[d - 1, e] = entry
    negate_imag(v_refs, nv_ref)
    for d in (0, 1):
        shift_plane(v_refs, sv_ref, d + 1)
        fill_hops(u_ref, d, sv_ref, h_ref)
        pack_products(gram(v_refs, nv_ref, h_ref), w_ref, 4 * d)


def x_kernel(parts, ux_ref, *refs):
    v_refs, near_ref, rest = refs[:parts], refs[parts], refs[parts + 1 :]
    done_refs, (out_ref, h_ref, nv_ref) = rest[:-3], rest[-3:]
    negate_imag(v_refs, nv_ref)
    fill_hops(ux_ref, 0, near_ref, h_ref)
    total = gram(v_refs, nv_ref, h_ref)
    if len(done_refs) == 0 and out_ref.ndim == 2:
        out_ref[...] = total
    else:
        pack_products(
            jnp.concatenate([r[...] for r in done_refs] + [total], 1), out_ref, 0
        )


def copy_to(src, dst, sems, row, step, device):
    return pltpu.make_async_remote_copy(
        src_ref=src,
        dst_ref=dst,
        send_sem=sems.at[row, step],
        recv_sem=sems.at[row + 1, step],
        device_id=device,
        device_id_type=MESH,
    )


def core_sum_kernel(w_ref, out_ref, got, sems):
    me = lax.axis_index("sx")
    core = lax.rem(me, 2)
    partner = (lax.axis_index("cfg"), (me // 2) * 2 + 1 - core)
    barrier = pltpu.get_barrier_semaphore()
    pl.semaphore_signal(barrier, inc=1, device_id=partner, device_id_type=MESH)
    pl.semaphore_wait(barrier, 1)
    copy = copy_to(w_ref.at[1 - core], got, sems, 0, 0, partner)
    copy.start()
    copy.wait()
    out_ref[...] = (w_ref[core] + got[...]).astype(BF16)


def sum_kernel(chips, w_ref, yz_ref, x_out, yz_out, got, send, came, mine, full, sems):
    me = lax.axis_index("sx")
    cfg = lax.axis_index("cfg")
    core = lax.rem(me, 2)
    chip = me // 2
    other = 1 - core
    partner = (cfg, chip * 2 + other)
    rows = w_ref.shape[2]

    def chip_at(step):
        return lax.rem(chip + step, chips)

    def same_core(step):
        return (cfg, chip_at(step) * 2 + core)

    barrier = pltpu.get_barrier_semaphore()
    pl.semaphore_signal(barrier, inc=1, device_id=partner, device_id_type=MESH)
    for step in range(1, chips):
        pl.semaphore_signal(
            barrier, inc=1, device_id=same_core(step), device_id_type=MESH
        )
    pl.semaphore_wait(barrier, chips)

    order = list(range(1, chips)) + [0]
    halves, pieces, back = {}, {}, {}
    for step in order:
        to = chip_at(step)
        halves[step] = copy_to(w_ref.at[other, to], got.at[to], sems, 0, step, partner)
        halves[step].start()
    for step in order[:-1]:
        to = chip_at(step)
        send[to, rows:] = yz_ref[to]
        halves[step].wait_recv()
        send[to, :rows] = (w_ref[core, to] + got[to]).astype(BF16)
        pieces[step] = copy_to(
            send.at[to], came.at[step], sems, 2, step, same_core(step)
        )
        pieces[step].start()
    halves[0].wait_recv()
    total = jnp.concatenate(
        [w_ref[core, chip] + got[chip], yz_ref[chip].astype(F32)], 0
    )
    for step in order[:-1]:
        pieces[step].wait_recv()
        total = total + came[step].astype(F32)
    mine[...] = total.astype(BF16)
    full[core, chip] = total.astype(BF16)

    for step in order[:-1]:
        back[step] = copy_to(mine, full.at[core, chip], sems, 4, step, same_core(step))
        back[step].start()
    passed = [copy_to(mine, full.at[core, chip], sems, 6, 0, partner)]
    passed[0].start()
    for step in order[:-1]:
        origin = lax.rem(chip + chips - step, chips)
        block = full.at[core, origin]
        back[step].wait_recv()
        passed.append(copy_to(block, block, sems, 6, step, partner))
        passed[-1].start()
    for copy in passed:
        copy.wait()
    for step in order:
        halves[step].wait_send()
    for step in order[:-1]:
        pieces[step].wait_send()
        back[step].wait_send()
    x_out[...] = full[:, :, :rows]
    yz_out[...] = full[:, :, rows:]


def split_rows(w):
    size = lax.axis_size("sx")
    blocks, rows, lanes = w.shape
    return w.reshape(2, size // 2, blocks * rows // size, lanes)


def sum_over_cores(w):
    parts = split_rows(w)
    vmem = pl.BlockSpec(memory_space=pltpu.VMEM)
    return pl.pallas_call(
        core_sum_kernel,
        out_shape=jax.ShapeDtypeStruct(parts.shape[1:], BF16),
        in_specs=[vmem],
        out_specs=vmem,
        scratch_shapes=[
            pltpu.VMEM(parts.shape[1:], F32),
            pltpu.SemaphoreType.DMA((2, 1)),
        ],
        compiler_params=pltpu.CompilerParams(
            collective_id=0, has_side_effects=True, vmem_limit_bytes=SMALL
        ),
        name="sum_over_cores",
    )(parts)


def sum_over_sites(w, part_yz):
    parts = split_rows(w)
    _, chips, rows, lanes = parts.shape
    rows_yz = part_yz.shape[1]
    both = (chips, rows + rows_yz, lanes)
    vmem = pl.BlockSpec(memory_space=pltpu.VMEM)
    x, yz = pl.pallas_call(
        functools.partial(sum_kernel, chips),
        out_shape=(
            jax.ShapeDtypeStruct((2, chips, rows, lanes), BF16),
            jax.ShapeDtypeStruct((2, chips, rows_yz, lanes), BF16),
        ),
        in_specs=[vmem] * 2,
        out_specs=(vmem, vmem),
        scratch_shapes=[
            pltpu.VMEM((chips, rows, lanes), F32),
            pltpu.VMEM(both, BF16),
            pltpu.VMEM(both, BF16),
            pltpu.VMEM(both[1:], BF16),
            pltpu.VMEM((2,) + both, BF16),
            pltpu.SemaphoreType.DMA((8, chips)),
        ],
        compiler_params=pltpu.CompilerParams(
            collective_id=1, has_side_effects=True, vmem_limit_bytes=SMALL
        ),
        name="sum_over_sites",
    )(parts, part_yz)
    return x.reshape(w.shape), yz.reshape(-1, *w.shape[1:])


def tiles_kernel(scale, slot_ref, x_ref, yz_ref, out_ref, m_ref):
    half = x_ref.shape[1]
    modes = 2 * half
    tiles = modes // TM
    count = 3
    slots, entries = out_ref.shape
    row = lax.broadcasted_iota(jnp.int32, (half, half), 0)
    col = lax.broadcasted_iota(jnp.int32, (half, half), 1)
    for n in range(count):
        src_ref, base = (x_ref, 0) if n == 0 else (yz_ref, 4 * n - 4)
        re_w = src_ref[base].astype(F32)
        im_w = src_ref[base + 2].astype(F32)
        re_t, im_t = re_w.T, im_w.T
        zero = jnp.zeros_like(re_w)
        re_top = jnp.where(row < col, re_w, jnp.where(row > col, -re_t, zero))
        re_low = jnp.where(row > col, re_w, jnp.where(row < col, -re_t, zero))
        im_top = jnp.where(row <= col, im_w, im_t)
        im_low = jnp.where(row > col, im_w, jnp.where(row < col, im_t, re_w))
        for t, top, low in ((0, re_top, re_low), (1, im_top, im_low)):
            at = (2 * n + t) * modes
            m_ref[:half, at : at + half] = top.astype(BF16)
            m_ref[:half, at + half : at + modes] = src_ref[base + 2 * t + 1]
            m_ref[half:, at : at + half] = zero.astype(BF16)
            m_ref[half:, at + half : at + modes] = low.astype(BF16)
    slot = slot_ref[...]
    mode = lax.broadcasted_iota(jnp.int32, (slots, modes), 1)
    i = mode // TM
    start = i * tiles - (i * (i - 1)) // 2
    in_row = (slot >= start) & (slot < start + tiles - i)
    i_of = jnp.max(jnp.where(in_row, i, 0), axis=1, keepdims=True)
    j_of = slot - (i_of * tiles - (i_of * (i_of - 1)) // 2) + i_of
    in_col = jnp.concatenate([(i == j_of).astype(F32)] * (2 * count), axis=1)
    wide = -(-entries // LANES) * LANES
    place_row = lax.broadcasted_iota(jnp.int32, (2 * count * modes, wide), 0)
    place_col = lax.broadcasted_iota(jnp.int32, (2 * count * modes, wide), 1)
    target = (place_row // modes) * (TM * TM) + place_row % TM
    place = (target == place_col).astype(F32).astype(BF16)
    total = jnp.zeros((slots, wide), F32)
    for r in range(TM):
        pick = (mode == i_of * TM + r).astype(F32).astype(BF16)
        rows = jnp.dot(pick, m_ref[...], preferred_element_type=F32)
        found = jnp.dot((rows * in_col).astype(BF16), place, preferred_element_type=F32)
        total = total + (found if r == 0 else pltpu.roll(found, TM * r, 1))
    out_ref[...] = total[:, :entries] * scale


def per_device(eigvecs, link_seed, ownership):
    modes, _, _, layers, sites = eigvecs.shape
    size = lax.axis_size("sx")
    me = lax.axis_index("sx")
    half = modes // 2
    part = modes // PARTS
    extent_x = layers * size
    v = [
        eigvecs[j * part : (j + 1) * part].transpose(1, 2, 3, 0, 4).reshape(6, part, sites)
        for j in range(PARTS)
    ]
    near = [from_behind(block, "sx", -1) for block in v]
    slots = ownership.shape[0] // size
    own = lax.dynamic_slice_in_dim(ownership, me * slots, slots).reshape(slots, 1)
    scale = 1.0 / math.sqrt(12.0 * extent_x * sites)
    vmem = pl.BlockSpec(memory_space=pltpu.VMEM)
    link_shape = (1, 18, sites // LANES, LANES)
    plane = (6, modes, sites)
    negated = pltpu.VMEM((3, modes, sites), BF16)
    large = pltpu.CompilerParams(vmem_limit_bytes=LARGE)
    small = pltpu.CompilerParams(vmem_limit_bytes=SMALL)

    w_yz, u_x = pl.pallas_call(
        yz_kernel,
        out_shape=(
            jax.ShapeDtypeStruct((8, half, half), F32),
            jax.ShapeDtypeStruct(link_shape, F32),
        ),
        in_specs=[pl.BlockSpec(memory_space=pltpu.SMEM)] + [vmem] * PARTS,
        out_specs=(vmem, vmem),
        scratch_shapes=[
            pltpu.VMEM((2,) + link_shape[1:], F32),
            pltpu.VMEM(plane, BF16),
            pltpu.VMEM(plane, BF16),
            negated,
        ],
        compiler_params=large,
        name="products_yz",
    )(link_seed, *v)
    part_yz = sum_over_cores(w_yz)
    done = []
    for j in range(PARTS):
        last = j == PARTS - 1
        shape = (4, half, half) if last else (2 * modes, part)
        operands = [u_x, *v, near[j]] + (done if last else [])
        done.append(
            pl.pallas_call(
                functools.partial(x_kernel, PARTS),
                out_shape=jax.ShapeDtypeStruct(shape, F32),
                in_specs=[vmem] * len(operands),
                out_specs=vmem,
                scratch_shapes=[pltpu.VMEM((6, part, sites), BF16), negated],
                compiler_params=large,
                name="products_x" + str(j),
            )(*operands)
        )
    sum_x, sum_yz = sum_over_sites(done[-1], part_yz)
    return pl.pallas_call(
        functools.partial(tiles_kernel, scale),
        out_shape=jax.ShapeDtypeStruct((slots, 6 * TM * TM), F32),
        in_specs=[vmem] * 3,
        out_specs=vmem,
        scratch_shapes=[pltpu.VMEM((modes, 6 * modes), BF16)],
        compiler_params=small,
        name="own_tiles",
    )(own, sum_x, sum_yz)


def solution(mesh):
    return jax.shard_map(
        per_device,
        mesh=mesh,
        in_specs=(P("cfg", None, None, "sx", None), P("cfg"), P()),
        out_specs=P(("cfg", "sx"), None),
        check_vma=False,
    )
```

profile of v0, /device:TPU:0, one launch (start us, length us, event | category | flops | bytes accessed | tf_op | source)
XLA Modules:
  0.0 69.8 jit_solution(4512855440658363658)
XLA Ops:
  0.0 3.9 %slice_bitcast_fusion = (bf16[2,3,1,128,1024]{4,0,2,1,3:T(2,128)(2,1)S(1)}, bf16[2,3,1,128,1024]{4,0,2,1,3:T(2,128)(2,1)S(1)}) fusion(bf16[256,2,3,1,1024]{4,1,3,2,0:T(2,128)(2,1)} %param.3), kind=kLoop, calls=%fused_computation | loop fusion | bytes 6291456 | tf_op jit(solution)/shard_map/transpose | solution.py:417
  3.9 0.5 copy.6
  4.3 5.5 %collective-permute-start.1 = (bf16[6,128,1024]{2,1,0:T(8,128)(2,1)S(1)}, bf16[6,128,1024]{2,1,0:T(8,128)(2,1)}, u32[]{:S(2)}, u32[]{:S(2)}) collective-permute-start(bf16[6,128,1024]{2,1,0:T(8,128)(2,1)S(1)} %bitcast.11), channel_id=1, source_target_pairs={{1,0},{2,1},{3,2},{4,3},{5,4},{6,5},{7,6},{8,7},{9,8},{10,9},{11,1... | collective-permute-start | bytes 4718600 | tf_op jit(solution)/shard_map/ppermute | solution.py:27
  9.8 0.0 copy-start
  9.8 0.5 copy.7
  10.3 0.7 %collective-permute-start = (bf16[6,128,1024]{2,1,0:T(8,128)(2,1)S(1)}, bf16[6,128,1024]{2,1,0:T(8,128)(2,1)}, u32[]{:S(2)}, u32[]{:S(2)}) collective-permute-start(bf16[6,128,1024]{2,1,0:T(8,128)(2,1)S(1)} %bitcast.15), channel_id=1, source_target_pairs={{1,0},{2,1},{3,2},{4,3},{5,4},{6,5},{7,6},{8,7},{9,8},{10,9},{11,1... | collective-permute-start | bytes 4718600 | tf_op jit(solution)/shard_map/ppermute | solution.py:27
  11.0 0.8 %dynamic_slice.3 = s32[130]{0:T(256)S(1)} dynamic-slice(s32[2080]{0:T(1024)} %param.5, s32[]{:T(128)S(6)} %select_n.3), dynamic_slice_sizes={130} | dynamic-slice | bytes 1044 | tf_op jit(solution)/shard_map/dynamic_slice | solution.py:422
  11.8 0.1 copy.8.slot_ref
  11.9 0.0 copy-done
  11.9 18.6 %products_yz.1 = (f32[8,128,128]{2,1,0:T(8,128)S(1)}, f32[1,18,8,128]{3,2,1,0:T(8,128)S(1)}) custom-call(s32[3]{0:T(128)S(1)} %copy-done, bf16[6,128,1024]{2,1,0:T(8,128)(2,1)S(1)} %bitcast.12, bf16[6,128,1024]{2,1,0:T(8,128)(2,1)S(1)} %bitcast.16), custom_call_target="tpu_custom_call" | custom-call | tf_op jit(solution)/shard_map/products_yz/pallas_call | solution.py:431
  30.5 1.6 %sum_over_cores.1.yz_ref = bf16[8,64,128]{2,1,0:T(8,128)(2,1)S(1)} custom-call(f32[2,8,64,128]{3,2,1,0:T(8,128)S(1)} %bitcast.20), custom_call_target="tpu_custom_call" | custom-call | tf_op jit(solution)/shard_map/sum_over_cores/pallas_call | solution.py:317
  32.1 0.0 collective-permute-done.1.refs_2_
  32.1 5.1 %products_x0.1.refs_3_ = f32[512,128]{1,0:T(8,128)S(1)} custom-call(f32[1,18,8,128]{3,2,1,0:T(8,128)S(1)} %get-tuple-element.9.ux_ref, bf16[6,128,1024]{2,1,0:T(8,128)(2,1)S(1)} %bitcast.13, bf16[6,128,1024]{2,1,0:T(8,128)(2,1)S(1)} %bitcast.17, bf16[6,128,1024]{2,1,0:T(8,128)(2,1)} %collective-permute-done.1.refs_2_), custom_call_target="tpu_custom_call" | custom-call | tf_op jit(solution)/shard_map/products_x0/pallas_call | solution.py:455
  37.2 7.4 %collective-permute-done.refs_2_ = bf16[6,128,1024]{2,1,0:T(8,128)(2,1)} collective-permute-done((bf16[6,128,1024]{2,1,0:T(8,128)(2,1)S(1)}, bf16[6,128,1024]{2,1,0:T(8,128)(2,1)}, u32[]{:S(2)}, u32[]{:S(2)}) %collective-permute-start) | collective-permute-done | bytes 1572896 | tf_op jit(solution)/shard_map/ppermute | solution.py:27
  44.6 5.2 %products_x1.1 = f32[4,128,128]{2,1,0:T(8,128)S(1)} custom-call(f32[1,18,8,128]{3,2,1,0:T(8,128)S(1)} %get-tuple-element.9.ux_ref, bf16[6,128,1024]{2,1,0:T(8,128)(2,1)S(1)} %bitcast.14, bf16[6,128,1024]{2,1,0:T(8,128)(2,1)S(1)} %bitcast.18, bf16[6,128,1024]{2,1,0:T(8,128)(2,1)} %collective-permute-done.refs_2_, f32[512,128]{1,0:T(8,128)S(1)} %products_x0.1.refs_3_), custom_call_target="tpu_custom_call" | custom-call | tf_op jit(solution)/shard_map/products_x1/pallas_call | solution.py:455
  49.8 17.7 %sum_over_sites.1 = (bf16[2,8,32,128]{3,2,1,0:T(8,128)(2,1)S(1)}, bf16[2,8,64,128]{3,2,1,0:T(8,128)(2,1)S(1)}) custom-call(f32[2,8,32,128]{3,2,1,0:T(8,128)S(1)} %bitcast.19, bf16[8,64,128]{2,1,0:T(8,128)(2,1)S(1)} %sum_over_cores.1.yz_ref), custom_call_target="tpu_custom_call" | custom-call | tf_op jit(solution)/shard_map/sum_over_sites/pallas_call | solution.py:339
  67.5 2.3 %own_tiles.1 = f32[130,96]{1,0:T(8,128)} custom-call(s32[130,1]{1,0:T(8,128)S(1)} %copy.8.slot_ref, bf16[4,128,128]{2,1,0:T(8,128)(2,1)S(1)} %bitcast.22, bf16[8,128,128]{2,1,0:T(8,128)(2,1)S(1)} %bitcast.21), custom_call_target="tpu_custom_call" | custom-call | tf_op jit(solution)/shard_map/own_tiles/pallas_call | solution.py:466
Async XLA Ops:
  4.3 27.8 %collective-permute-start.1 = (bf16[6,128,1024]{2,1,0:T(8,128)(2,1)S(1)}, bf16[6,128,1024]{2,1,0:T(8,128)(2,1)}, u32[]{:S(2)}, u32[]{:S(2)}) collective-permute-start(bf16[6,128,1024]{2,1,0:T(8,128)(2,1)S(1)} %bitcast.11), channel_id=1, source_target_pairs={{1,0},{2,1},{3,2},{4,3},{5,4},{6,5},{7,6},{8,7},{9,8},{10,9},{11,1... | collective-permute-start | bytes 4718600 | tf_op jit(solution)/shard_map/ppermute | solution.py:27
  9.8 2.1 %copy-start = (s32[3]{0:T(128)S(1)}, s32[3]{0:T(128)}, u32[]{:S(2)}) copy-start(s32[3]{0:T(128)} %seed_ref.1) | copy-start | bytes 40
  10.3 34.3 %collective-permute-start = (bf16[6,128,1024]{2,1,0:T(8,128)(2,1)S(1)}, bf16[6,128,1024]{2,1,0:T(8,128)(2,1)}, u32[]{:S(2)}, u32[]{:S(2)}) collective-permute-start(bf16[6,128,1024]{2,1,0:T(8,128)(2,1)S(1)} %bitcast.15), channel_id=1, source_target_pairs={{1,0},{2,1},{3,2},{4,3},{5,4},{6,5},{7,6},{8,7},{9,8},{10,9},{11,1... | collective-permute-start | bytes 4718600 | tf_op jit(solution)/shard_map/ppermute | solution.py:27
where the time goes:
time: 70 us; the launch traced here: 69.8 us
  Pallas kernels  50.4 us (72%)
  waiting for transfers between devices  7.42 us (11%)
  starting transfers between devices  6.23 us (9%)
  local copies, waits for them, and re-layouts  5.66 us (8%)
    pallas_call x1, Pallas kernels, per_device(): pl.pallas_call(yz_kernel, out_shape=(jax.ShapeDtypeStruct((8, half, half)...  18.6 us
    pallas_call x1, Pallas kernels, sum_over_sites(): pl.pallas_call(functools.partial(sum_kernel, chips), out_shape=(jax.Shape...  17.7 us
    pallas_call x2, Pallas kernels, per_device(): pl.pallas_call(functools.partial(x_kernel, PARTS), out_shape=jax.ShapeDty...  10.3 us
    ppermute x2, waiting for transfers between devices, from_behind(): return lax.ppermute(block, axis, route)  7.42 us
    ppermute x2, starting transfers between devices, from_behind(): return lax.ppermute(block, axis, route)  6.23 us
    transpose x3, local copies, waits for them, and re-layouts, per_device(): eigvecs[j * part:(j + 1) * part].transpose(1, 2, 3, 0, 4)  4.78 us
    pallas_call x1, Pallas kernels, per_device(): pl.pallas_call(functools.partial(tiles_kernel, scale), out_shape=jax.Shap...  2.27 us
    pallas_call x1, Pallas kernels, sum_over_cores(): pl.pallas_call(core_sum_kernel, out_shape=jax.ShapeDtypeStruct(parts.shap...  1.62 us
  transfers between devices with their start and end apart: 2, of which 1 were waited for; matrix products, arithmetic and copies ran while one was open for 2% of the time, Pallas kernels for 36%

commit v1 on v0

v1 whole, which is shorter than its diff:
```python
import functools
import math

import jax
import jax.numpy as jnp
from jax import lax
from jax.experimental import pallas as pl
from jax.experimental.pallas import tpu as pltpu
from jax.sharding import PartitionSpec as P

TM = 4
NZ = 64
MODULUS = 46337
LANES = 128
ROWS = 16
COLOURS = 3
LARGE = 48 * 1024 * 1024
MESH = pl.DeviceIdType.MESH
F32 = jnp.float32
BF16 = jnp.bfloat16
NT = (((1,), (1,)), ((), ()))


def quotient(value):
    q = jnp.floor(value.astype(F32) * (1.0 / MODULUS)).astype(jnp.int32)
    rest = value - q * MODULUS
    q = jnp.where(rest < 0, q - 1, jnp.where(rest >= MODULUS, q + 1, q))
    return q


def modulo(value):
    return value - quotient(value) * MODULUS


def links(seed, first_site, shape):
    code = (
        first_site
        + lax.broadcasted_iota(jnp.int32, shape, 0) * LANES
        + lax.broadcasted_iota(jnp.int32, shape, 1)
    )
    high = quotient(code)
    low = code - high * MODULUS
    mixed = modulo(seed * seed + low)
    mixed = modulo(mixed * mixed + high * 977 + 31)
    th = []
    for k in range(7):
        g = modulo(mixed + (5171 * k + 1))
        g = modulo(g * g + low)
        g = modulo(g * g + 12345)
        th.append(g.astype(F32) * (2.0 * math.pi / MODULUS) - math.pi)
    ca, sa = jnp.cos(th[0]), jnp.sin(th[0])
    cb, sb = jnp.cos(th[1]), jnp.sin(th[1])
    cg, sg = jnp.cos(th[2]), jnp.sin(th[2])
    rot = [
        [ca * cb * cg - sa * sg, -ca * cb * sg - sa * cg, ca * sb],
        [sa * cb * cg + ca * sg, -sa * cb * sg + ca * cg, sa * sb],
        [-sb * cg, sb * sg, cb],
    ]
    left = [th[3], th[4], -th[3] - th[4]]
    right = [th[5], th[6], -th[5] - th[6]]
    real, imag = [], []
    for r in range(3):
        for c in range(3):
            angle = left[r] + right[c]
            real.append(rot[r][c] * jnp.cos(angle))
            imag.append(rot[r][c] * jnp.sin(angle))
    return real + imag


def fill_hops(u_ref, d, src_ref, site, h_ref, slot):
    blocks, _, rows_all, _ = src_ref.shape
    after = lax.rem(site + 1, blocks)
    row = lax.broadcasted_iota(jnp.int32, (8, LANES), 0)
    lane = lax.broadcasted_iota(jnp.int32, (8, LANES), 1)
    even = row % 2 == 0
    sign = jnp.where(even, -1.0, 1.0).astype(F32)
    first_half = lane < NZ
    last = lane % NZ == NZ - 1

    def entry(e):
        return jnp.broadcast_to(u_ref[d, e, pl.ds(site, 1), :], (8, LANES))

    ur = [entry(e) for e in range(9)]
    ui = [entry(9 + e) * sign for e in range(9)]

    def rows_step(g, carry):
        rows = pl.ds(pl.multiple_of(g * ROWS, ROWS), ROWS)
        here = [src_ref[site, c, rows].astype(F32) for c in range(COLOURS)]
        if d == 1:
            there = [src_ref[after, c, rows].astype(F32) for c in range(COLOURS)]
        out = [[], [], []]
        for lo in (0, 8):
            v, s = [], []
            for c in range(COLOURS):
                x = here[c][lo : lo + 8]
                if d == 1:
                    x = jnp.where(first_half, there[c][lo : lo + 8], x)
                    x = pltpu.roll(x, LANES - NZ, 1)
                elif d == 2:
                    x = jnp.where(
                        last, pltpu.roll(x, NZ - 1, 1), pltpu.roll(x, LANES - 1, 1)
                    )
                v.append(x)
                s.append(jnp.where(even, pltpu.roll(x, 7, 0), pltpu.roll(x, 1, 0)))
            for c in range(COLOURS):
                total = None
                for k in range(COLOURS):
                    term = ur[3 * c + k] * v[k] + ui[3 * c + k] * s[k]
                    total = term if total is None else total + term
                out[c].append(total)
        for c in range(COLOURS):
            h_ref[slot, c, rows] = jnp.concatenate(out[c], 0).astype(BF16)
        return carry

    lax.fori_loop(0, rows_all // ROWS, rows_step, 0, unroll=2)


def add_products(v_ref, sites, h_ref, g_ref):
    left = jnp.concatenate(
        [v_ref[site, c] for site in sites for c in range(COLOURS)], 1
    )
    right = jnp.concatenate(
        [h_ref[slot, c] for slot in range(len(sites)) for c in range(COLOURS)], 1
    )
    g_ref[...] += lax.dot_general(left, right, NT, preferred_element_type=F32)


def derive(g_ref, c_ref, e_ref):
    both = g_ref.shape[0]
    modes = both // 2
    lane = lax.broadcasted_iota(jnp.int32, (modes, LANES), 1)
    even = lane % 2 == 0
    for n, j in enumerate(range(0, both, LANES)):
        for i in range(0, j + LANES, LANES):
            c_ref[n, i : i + LANES] = (
                g_ref[i : i + LANES, j : j + LANES]
                - g_ref[j : j + LANES, i : i + LANES].T
            )
        re_row = c_ref[n, pl.ds(0, modes, stride=2), :]
        im_row = c_ref[n, pl.ds(1, modes, stride=2), :]
        other = jnp.where(
            even, pltpu.roll(im_row, LANES - 1, 1), -pltpu.roll(im_row, 1, 1)
        )
        e_ref[:, j : j + LANES] = re_row + other


def prepare_slots(slot_ref, core, pad_ref, pick_ref, mask_ref, place_ref):
    devices, slots = slot_ref.shape
    rows = pad_ref.shape[1]
    modes = pick_ref.shape[2]
    tiles = modes // TM
    pad_ref[...] = jnp.full(pad_ref.shape, -1.0, F32)
    pad_ref[:, :slots] = slot_ref[...].astype(F32)
    columns = pad_ref[...].T
    mode = lax.broadcasted_iota(jnp.int32, (rows, modes), 1)
    i = mode // TM
    start = i * tiles - (i * (i - 1)) // 2
    lane = lax.broadcasted_iota(jnp.int32, (rows, 2 * modes), 1)
    for chip in range(devices // 2):
        pair = columns[:, 2 * chip : 2 * chip + 2]
        slot = jnp.where(core == 0, pair[:, :1], pair[:, 1:]).astype(jnp.int32)
        in_row = (slot >= start) & (slot < start + tiles - i)
        at = slice(chip * rows, (chip + 1) * rows)
        for r in range(TM):
            pick = jnp.where(in_row & (mode % TM == r), 1.0, 0.0)
            pick_ref[r, at] = pick.astype(BF16)
        i_of = jnp.max(jnp.where(in_row, i, 0), axis=1, keepdims=True)
        j_of = slot - (i_of * tiles - (i_of * (i_of - 1)) // 2) + i_of
        mask_ref[at] = jnp.where(lane // (2 * TM) == j_of, 1.0, 0.0)
    row = lax.broadcasted_iota(jnp.int32, (2 * modes, LANES), 0)
    col = lax.broadcasted_iota(jnp.int32, (2 * modes, LANES), 1)
    for d in range(3):
        for r in range(TM):
            target = ((2 * d + row % 2) * TM + r) * TM + (row // 2) % TM
            at = slice(r * 2 * modes, (r + 1) * 2 * modes)
            place_ref[d, at] = jnp.where(target == col, 1.0, 0.0).astype(BF16)


def main_kernel(
    scale,
    seed_ref,
    slot_ref,
    raw_ref,
    out_ref,
    own_ref,
    near_ref,
    u_ref,
    h_ref,
    g_ref,
    c_ref,
    e_ref,
    swap_ref,
    got_ref,
    sum_ref,
    pad_ref,
    pick_ref,
    mask_ref,
    place_ref,
    acc_ref,
    send_ref,
    came_ref,
    local_sems,
    plane_sems,
    swap_sems,
    piece_sems,
):
    cfg = lax.axis_index("cfg")
    me = lax.axis_index("sx")
    size = lax.axis_size("sx")
    chips = size // 2
    core = lax.rem(me, 2)
    chip = me // 2
    partner = (cfg, chip * 2 + 1 - core)
    below = (cfg, lax.rem(me + size - 1, size))
    modes, _, blocks, _, _ = raw_ref.shape
    rows = pad_ref.shape[1]
    slots, entries = out_ref.shape

    barrier = pltpu.get_barrier_semaphore()
    for step in range(1, size):
        pl.semaphore_signal(
            barrier,
            inc=1,
            device_id=(cfg, lax.rem(me + step, size)),
            device_id_type=MESH,
        )
    local = []
    for k in range(blocks):
        for c in range(COLOURS):
            local.append(
                pltpu.make_async_copy(
                    raw_ref.at[:, c, k], own_ref.at[k, c], local_sems.at[k, c]
                )
            )
            local[-1].start()
    first = me * (blocks * LANES)
    for d in (1, 2, 0):
        for e, value in enumerate(links(seed_ref[d], first, (blocks, LANES))):
            u_ref[d, e] = value
    pl.semaphore_wait(barrier, size - 1)
    planes = []
    for k in range(blocks):
        for c in range(COLOURS):
            local[k * COLOURS + c].wait()
        planes.append(
            pltpu.make_async_remote_copy(
                src_ref=own_ref.at[k],
                dst_ref=near_ref.at[k],
                send_sem=plane_sems.at[0, k],
                recv_sem=plane_sems.at[1, k],
                device_id=below,
                device_id_type=MESH,
            )
        )
        planes[-1].start()

    v = own_ref.reshape(blocks, COLOURS, 2 * modes, LANES)
    near = near_ref.reshape(blocks, COLOURS, 2 * modes, LANES)
    c_ref[...] = jnp.zeros_like(c_ref)
    swaps = {}

    def finish(d):
        derive(g_ref, c_ref, e_ref.at[d])
        swap_ref[d] = e_ref[d].astype(BF16)
        swaps[d] = pltpu.make_async_remote_copy(
            src_ref=swap_ref.at[d],
            dst_ref=got_ref.at[d],
            send_sem=swap_sems.at[0, d],
            recv_sem=swap_sems.at[1, d],
            device_id=partner,
            device_id_type=MESH,
        )
        swaps[d].start()

    def gather(d, at):
        found = []
        for r in range(TM):
            line = jnp.dot(
                pick_ref[r, at], sum_ref[...], preferred_element_type=F32
            )
            found.append((line * mask_ref[at]).astype(BF16))
        return jnp.dot(
            jnp.concatenate(found, 1), place_ref[d], preferred_element_type=F32
        )

    def piece_rows(to):
        return pl.ds(pl.multiple_of(to * rows, rows), rows)

    for d in (1, 2):
        g_ref[...] = jnp.zeros_like(g_ref)

        def pair_step(k, carry, d=d):
            sites = (2 * k, 2 * k + 1)
            for slot, site in enumerate(sites):
                fill_hops(u_ref, d, v, site, h_ref, slot)
            add_products(v, sites, h_ref, g_ref)
            return carry

        lax.fori_loop(0, blocks // 2, pair_step, 0)
        finish(d)

    prepare_slots(slot_ref, core, pad_ref, pick_ref, mask_ref, place_ref)
    for d in (1, 2):
        swaps[d].wait()
        sum_ref[...] = (e_ref[d] + got_ref[d].astype(F32)).astype(BF16)

        def spread_step(to, carry, d=d):
            at = piece_rows(to)
            found = gather(d, at)
            acc_ref[at] = found if d == 1 else acc_ref[at] + found
            return carry

        lax.fori_loop(0, chips, spread_step, 0)

    g_ref[...] = jnp.zeros_like(g_ref)

    def arrived(k):
        return pltpu.make_async_remote_copy(
            src_ref=own_ref.at[k],
            dst_ref=near_ref.at[k],
            send_sem=plane_sems.at[0, k],
            recv_sem=plane_sems.at[1, k],
            device_id=below,
            device_id_type=MESH,
        )

    def near_step(k, carry):
        sites = (2 * k, 2 * k + 1)
        for slot, site in enumerate(sites):
            arrived(site).wait_recv()
            fill_hops(u_ref, 0, near, site, h_ref, slot)
        add_products(v, sites, h_ref, g_ref)
        return carry

    lax.fori_loop(0, blocks // 2 - 1, near_step, 0)

    def last_step(k, carry):
        arrived(k).wait_recv()
        fill_hops(u_ref, 0, near, k, h_ref, 0)
        add_products(v, (k,), h_ref, g_ref)
        return carry

    lax.fori_loop(blocks - 2, blocks, last_step, 0)
    finish(0)
    swaps[0].wait()
    sum_ref[...] = (e_ref[0] + got_ref[0].astype(F32)).astype(BF16)

    def piece(step):
        to = lax.rem(chip + step, chips)
        return pltpu.make_async_remote_copy(
            src_ref=send_ref.at[to],
            dst_ref=came_ref.at[step],
            send_sem=piece_sems.at[0, step],
            recv_sem=piece_sems.at[1, step],
            device_id=(cfg, to * 2 + core),
            device_id_type=MESH,
        )

    def send_step(step, carry):
        to = lax.rem(chip + step, chips)
        at = piece_rows(to)
        send_ref[to] = (acc_ref[at] + gather(0, at)).astype(BF16)
        piece(step).start()
        return carry

    lax.fori_loop(1, chips, send_step, 0)
    at = piece_rows(chip)
    total = acc_ref[at] + gather(0, at)
    for step in range(1, chips):
        piece(step).wait_recv()
        total = total + came_ref[step].astype(F32)
    out_ref[...] = total[:slots, :entries] * scale
    for step in range(1, chips):
        piece(step).wait_send()
    for k in range(blocks):
        planes[k].wait_send()


def per_device(eigvecs, link_seed, ownership):
    modes, _, colours, layers, sites = eigvecs.shape
    size = lax.axis_size("sx")
    chips = size // 2
    blocks = sites // LANES
    raw = (
        eigvecs.transpose(0, 2, 3, 1, 4)
        .reshape(modes, colours, 2, blocks, LANES)
        .transpose(0, 1, 3, 2, 4)
    )
    slots = ownership.shape[0] // size
    rows = -(-slots // ROWS) * ROWS
    scale = 1.0 / math.sqrt(12.0 * layers * size * sites)
    vmem = pl.BlockSpec(memory_space=pltpu.VMEM)
    plane = pltpu.VMEM((blocks, colours, modes, 2, LANES), BF16)
    both = 2 * modes
    return pl.pallas_call(
        functools.partial(main_kernel, scale),
        out_shape=jax.ShapeDtypeStruct((slots, 6 * TM * TM), F32),
        in_specs=[
            pl.BlockSpec(memory_space=pltpu.SMEM),
            vmem,
            pl.BlockSpec(memory_space=pltpu.HBM),
        ],
        out_specs=vmem,
        scratch_shapes=[
            plane,
            plane,
            pltpu.VMEM((3, 18, blocks, LANES), F32),
            pltpu.VMEM((2, colours, both, LANES), BF16),
            pltpu.VMEM((both, both), F32),
            pltpu.VMEM((both // LANES, both, LANES), F32),
            pltpu.VMEM((3, modes, both), F32),
            pltpu.VMEM((3, modes, both), BF16),
            pltpu.VMEM((3, modes, both), BF16),
            pltpu.VMEM((modes, both), BF16),
            pltpu.VMEM((size, rows), F32),
            pltpu.VMEM((TM, chips * rows, modes), BF16),
            pltpu.VMEM((chips * rows, both), F32),
            pltpu.VMEM((3, TM * both, LANES), BF16),
            pltpu.VMEM((chips * rows, LANES), F32),
            pltpu.VMEM((chips, rows, LANES), BF16),
            pltpu.VMEM((chips, rows, LANES), BF16),
            pltpu.SemaphoreType.DMA((blocks, colours)),
            pltpu.SemaphoreType.DMA((2, blocks)),
            pltpu.SemaphoreType.DMA((2, 3)),
            pltpu.SemaphoreType.DMA((2, chips)),
        ],
        compiler_params=pltpu.CompilerParams(
            collective_id=0, has_side_effects=True, vmem_limit_bytes=LARGE
        ),
        name="elementals",
    )(link_seed, ownership.reshape(size, slots), raw)


def solution(mesh):
    return jax.shard_map(
        per_device,
        mesh=mesh,
        in_specs=(P("cfg", None, None, "sx", None), P("cfg"), P()),
        out_specs=P(("cfg", "sx"), None),
        check_vma=False,
    )
```

time: 70 us -> 76.5 us (1.093)
  Pallas kernels: 50.4 us -> 72.2 us
  waiting for transfers between devices: 7.42 us -> 0 us
  starting transfers between devices: 6.23 us -> 0 us
  local copies, waits for them, and re-layouts: 5.66 us -> 3.97 us
    pallas_call x6 -> x1, Pallas kernels: 50.4 us -> 72.2 us  [per_device(): pl.pallas_call(functools.partial(main_kernel, scale), out_shape=jax.Shape...]
    ppermute x2 -> x0, waiting for transfers between devices: 7.42 us -> none  [from_behind(): return lax.ppermute(block, axis, route)]
    ppermute x2 -> x0, starting transfers between devices: 6.23 us -> none  [from_behind(): return lax.ppermute(block, axis, route)]
    transpose x3 -> x0, local copies, waits for them, and re-layouts: 4.78 us -> none  [per_device(): eigvecs[j * part:(j + 1) * part].transpose(1, 2, 3, 0, 4)]
    unnamed x2 -> x5, local copies, waits for them, and re-layouts: 0.01 us -> 3.17 us
    dynamic_slice x1 -> x0, local copies, waits for them, and re-layouts: 0.77 us -> none  [per_device(): lax.dynamic_slice_in_dim(ownership, me * slots, slots).reshape(slots, 1)]
  transfers between devices with their start and end apart: 2 -> 0, of which waited for: 1 -> 0; matrix products, arithmetic and copies ran while one was open for 2% -> 0% of each run, Pallas kernels for 36% -> 0%
where the time goes in v1:
time: 76.5 us; the launch traced here: 76.2 us
  Pallas kernels  72.2 us (94%)
  local copies, waits for them, and re-layouts  3.97 us (5%)
    pallas_call x1, Pallas kernels, per_device(): pl.pallas_call(functools.partial(main_kernel, scale), out_shape=jax.Shape...  72.2 us
    unnamed x5, local copies, waits for them, and re-layouts  3.17 us

profile of v1, /device:TPU:0, one launch (start us, length us, event | category | flops | bytes accessed | tf_op | source)
XLA Modules:
  0.0 76.2 jit_solution(1060408979944321988)
XLA Ops:
  0.0 0.8 %reshape.6.slot_ref = s32[16,130]{1,0:T(8,128)S(1)} reshape(s32[2080]{0:T(1024)} %param.5) | data formatting | bytes 16640 | tf_op jit(solution)/shard_map/reshape | solution.py:431
  0.8 0.0 copy-start
  0.8 1.9 %copy-done = bf16[256,2,3,1,1024]{4,1,3,2,0:T(2,128)(2,1)S(1)} copy-done((bf16[256,2,3,1,1024]{4,1,3,2,0:T(2,128)(2,1)S(1)}, bf16[256,2,3,1,1024]{4,1,3,2,0:T(2,128)(2,1)}, u32[]{:S(2)}) %copy-start) | copy-done | bytes 3145752
  2.7 0.0 copy-start.1
  2.7 0.7 copy-done.1
  3.4 72.2 %elementals.1 = f32[130,96]{1,0:T(8,128)S(1)} custom-call(s32[3]{0:T(128)S(1)} %copy-done.1, s32[16,130]{1,0:T(8,128)S(1)} %reshape.6.slot_ref, bf16[256,3,8,2,128]{4,3,2,1,0:T(2,128)(2,1)S(1)} %bitcast.5), custom_call_target="tpu_custom_call" | custom-call | tf_op jit(solution)/shard_map/elementals/pallas_call | solution.py:395
  75.6 0.6 copy.5
Async XLA Ops:
  0.8 1.9 %copy-start = (bf16[256,2,3,1,1024]{4,1,3,2,0:T(2,128)(2,1)S(1)}, bf16[256,2,3,1,1024]{4,1,3,2,0:T(2,128)(2,1)}, u32[]{:S(2)}) copy-start(bf16[256,2,3,1,1024]{4,1,3,2,0:T(2,128)(2,1)} %param.3) | copy-start | bytes 9437188
  2.7 0.7 copy-start.1

commit v2 on v1

v2 whole, which is shorter than its diff:
```python
import functools
import math

import jax
import jax.numpy as jnp
from jax import lax
from jax.experimental import pallas as pl
from jax.experimental.pallas import tpu as pltpu
from jax.sharding import PartitionSpec as P

TM = 4
NZ = 64
MODULUS = 46337
LANES = 128
ROWS = 16
COLOURS = 3
LARGE = 62 * 1024 * 1024
MESH = pl.DeviceIdType.MESH
F32 = jnp.float32
BF16 = jnp.bfloat16
NT = (((1,), (1,)), ((), ()))


def quotient(value):
    q = jnp.floor(value.astype(F32) * (1.0 / MODULUS)).astype(jnp.int32)
    rest = value - q * MODULUS
    q = jnp.where(rest < 0, q - 1, jnp.where(rest >= MODULUS, q + 1, q))
    return q


def modulo(value):
    return value - quotient(value) * MODULUS


def links(seed, code):
    high = quotient(code)
    low = code - high * MODULUS
    mixed = modulo(seed * seed + low)
    mixed = modulo(mixed * mixed + high * 977 + 31)
    th = []
    for k in range(7):
        g = modulo(mixed + (5171 * k + 1))
        g = modulo(g * g + low)
        g = modulo(g * g + 12345)
        th.append(g.astype(F32) * (2.0 * math.pi / MODULUS) - math.pi)
    ca, sa = jnp.cos(th[0]), jnp.sin(th[0])
    cb, sb = jnp.cos(th[1]), jnp.sin(th[1])
    cg, sg = jnp.cos(th[2]), jnp.sin(th[2])
    rot = [
        [ca * cb * cg - sa * sg, -ca * cb * sg - sa * cg, ca * sb],
        [sa * cb * cg + ca * sg, -sa * cb * sg + ca * cg, sa * sb],
        [-sb * cg, sb * sg, cb],
    ]
    left = [th[3], th[4], -th[3] - th[4]]
    right = [th[5], th[6], -th[5] - th[6]]
    real, imag = [], []
    for r in range(3):
        for c in range(3):
            angle = left[r] + right[c]
            real.append(rot[r][c] * jnp.cos(angle))
            imag.append(rot[r][c] * jnp.sin(angle))
    return real + imag


def behind(place, d, sites):
    if d == 1:
        return jnp.where(place < NZ, place + (sites - NZ), place - NZ)
    if d == 2:
        return jnp.where(place % NZ == 0, place + (NZ - 1), place - 1)
    return place


def shift_modes(v_ref, y_ref, z_ref):
    blocks = v_ref.shape[0]
    wide = 2 * LANES
    row = lax.broadcasted_iota(jnp.int32, (wide, LANES), 0)
    col = lax.broadcasted_iota(jnp.int32, (wide, LANES), 1)
    move_y = (row == col + (LANES - NZ)).astype(F32).astype(BF16)
    row = lax.broadcasted_iota(jnp.int32, (wide, wide), 0)
    col = lax.broadcasted_iota(jnp.int32, (wide, wide), 1)
    move_z = (row == behind(col, 2, wide)).astype(F32).astype(BF16)

    def step(k, carry):
        before = lax.rem(k + blocks - 1, blocks)
        for c in range(COLOURS):
            both = jnp.concatenate([v_ref[before, c], v_ref[k, c]], 1)
            moved = jnp.dot(both, move_y, preferred_element_type=F32)
            y_ref[k, c] = moved.astype(BF16)
        return carry

    def pair_step(k, carry):
        for c in range(COLOURS):
            both = jnp.concatenate([v_ref[2 * k, c], v_ref[2 * k + 1, c]], 1)
            moved = jnp.dot(both, move_z, preferred_element_type=F32).astype(BF16)
            z_ref[2 * k, c] = moved[:, :LANES]
            z_ref[2 * k + 1, c] = moved[:, LANES:]
        return carry

    lax.fori_loop(0, blocks, step, 0)
    lax.fori_loop(0, blocks // 2, pair_step, 0)


def widen(src_ref, site, f_ref):
    for c in range(COLOURS):
        f_ref[c] = src_ref[site, c].astype(F32)


def fill_hops(u_ref, d, f_ref, site, h_ref, slot):
    modes = f_ref.shape[1] // 2

    def entry(e):
        return jnp.broadcast_to(u_ref[d, e, pl.ds(site, 1), :], (8, LANES))

    u = [entry(e) for e in range(18)]

    def rows_step(g, carry):
        out = [[] for _ in range(6)]
        for lo in (0, 8):
            v = []
            for t in range(2):
                at = pl.multiple_of(2 * g * ROWS, 2 * ROWS) + 2 * lo + t
                for c in range(COLOURS):
                    v.append(f_ref[c, pl.ds(at, 8, stride=2), :])
            for c in range(COLOURS):
                re = im = None
                for k in range(COLOURS):
                    ur, ui = u[3 * c + k], u[9 + 3 * c + k]
                    p = ur * v[k] - ui * v[3 + k]
                    q = ur * v[3 + k] + ui * v[k]
                    re = p if re is None else re + p
                    im = q if im is None else im + q
                out[c].append(re)
                out[3 + c].append(im)
        for q in range(6):
            at = pl.multiple_of((q // 3) * modes + g * ROWS, ROWS)
            both = jnp.concatenate(out[q], 0).astype(BF16)
            h_ref[slot, q % 3, pl.ds(at, ROWS)] = both
        return carry

    lax.fori_loop(0, modes // ROWS, rows_step, 0, unroll=2)


def add_products(w_ref, sites, h_ref, g_ref):
    left = jnp.concatenate(
        [w_ref[site, c] for site in sites for c in range(COLOURS)], 1
    )
    right = jnp.concatenate(
        [h_ref[slot, c] for slot in range(len(sites)) for c in range(COLOURS)], 1
    )
    term = lax.dot_general(left, right, NT, preferred_element_type=F32)
    for n in range(g_ref.shape[0]):
        g_ref[n] += term[:, n * LANES : (n + 1) * LANES]


def derive(g_ref, s_ref, e_ref):
    parts, both, _ = g_ref.shape
    modes = both // 2
    count = parts // 2
    for n in range(count):
        here = [g_ref[n, pl.ds(t, modes, stride=2), :] for t in range(2)]
        there = [g_ref[count + n, pl.ds(t, modes, stride=2), :] for t in range(2)]
        s_ref[0, n] = here[0] + there[1]
        s_ref[1, n] = there[0] - here[1]
    for j in range(count):
        for i in range(j + 1):
            rows, cols = slice(i * LANES, (i + 1) * LANES), slice(j * LANES, (j + 1) * LANES)
            at = j * LANES
            e_ref[rows, at : at + LANES] = (
                s_ref[0, j, rows] - s_ref[0, i, cols].T
            ).astype(BF16)
            e_ref[rows, modes + at : modes + at + LANES] = (
                s_ref[1, j, rows] + s_ref[1, i, cols].T
            ).astype(BF16)


def prepare_slots(slot_ref, core, flat_ref, pick_ref, mask_ref, part_ref, place_ref):
    count = slot_ref.shape[1]
    chips, rows, modes = pick_ref.shape[0], pick_ref.shape[1] // TM, pick_ref.shape[2]
    tiles = modes // TM
    slots = count // (2 * chips)
    flat_ref[...] = jnp.full(flat_ref.shape, -1.0, F32)
    flat_ref[:, :count] = jnp.broadcast_to(slot_ref[...].astype(F32), (8, count))
    column = flat_ref[...].T[:, :1]
    mode = lax.broadcasted_iota(jnp.int32, (rows, modes), 1)
    i = mode // TM
    start = i * tiles - (i * (i - 1)) // 2
    lane = lax.broadcasted_iota(jnp.int32, (rows, LANES), 1)
    for chip in range(chips):
        at = 2 * chip * slots
        slot = jnp.where(
            core == 0, column[at : at + rows], column[at + slots : at + slots + rows]
        ).astype(jnp.int32)
        in_row = (slot >= start) & (slot < start + tiles - i)
        for r in range(TM):
            pick = jnp.where(in_row & (mode % TM == r), 1.0, 0.0)
            pick_ref[chip, r * rows : (r + 1) * rows] = pick.astype(BF16)
        i_of = jnp.max(jnp.where(in_row, i, 0), axis=1, keepdims=True)
        j_of = slot - (i_of * tiles - (i_of * (i_of - 1)) // 2) + i_of
        block = j_of // (LANES // TM)
        inside = j_of - block * (LANES // TM)
        part_ref[chip] = jnp.broadcast_to(block, (rows, LANES))
        mask_ref[chip] = jnp.where(lane // TM == inside, 1.0, 0.0)
    row = lax.broadcasted_iota(jnp.int32, (2 * TM * LANES, LANES), 0)
    col = lax.broadcasted_iota(jnp.int32, (2 * TM * LANES, LANES), 1)
    for d in range(3):
        r, t = row // (2 * LANES), (row // LANES) % 2
        target = ((2 * d + t) * TM + r) * TM + row % TM
        place_ref[d] = jnp.where(target == col, 1.0, 0.0).astype(BF16)


def main_kernel(
    scale,
    seed_ref,
    slot_ref,
    raw_ref,
    out_ref,
    own_ref,
    near_ref,
    y_ref,
    z_ref,
    u_ref,
    f_ref,
    h_ref,
    g_ref,
    s_ref,
    swap_ref,
    got_ref,
    sum_ref,
    flat_ref,
    pick_ref,
    mask_ref,
    part_ref,
    place_ref,
    acc_ref,
    send_ref,
    came_ref,
    slots_here,
    seeds_here,
    local_sems,
    small_sems,
    plane_sems,
    swap_sems,
    piece_sems,
):
    cfg = lax.axis_index("cfg")
    me = lax.axis_index("sx")
    size = lax.axis_size("sx")
    chips = size // 2
    core = lax.rem(me, 2)
    chip = me // 2
    partner = (cfg, chip * 2 + 1 - core)
    below = (cfg, lax.rem(me + size - 1, size))
    modes, _, blocks, _, _ = raw_ref.shape
    rows = send_ref.shape[1]
    slots, entries = out_ref.shape

    barrier = pltpu.get_barrier_semaphore()
    for step in range(1, size):
        pl.semaphore_signal(
            barrier,
            inc=1,
            device_id=(cfg, lax.rem(me + step, size)),
            device_id_type=MESH,
        )
    seed_copy = pltpu.make_async_copy(seed_ref, seeds_here, small_sems.at[0])
    seed_copy.start()
    local = []
    for k in range(blocks):
        for c in range(COLOURS):
            local.append(
                pltpu.make_async_copy(
                    raw_ref.at[:, c, k], own_ref.at[k, c], local_sems.at[k, c]
                )
            )
            local[-1].start()
    slot_copy = pltpu.make_async_copy(slot_ref, slots_here, small_sems.at[1])
    slot_copy.start()
    first = me * (blocks * LANES)
    position = lax.broadcasted_iota(
        jnp.int32, (blocks, LANES), 0
    ) * LANES + lax.broadcasted_iota(jnp.int32, (blocks, LANES), 1)
    seed_copy.wait()
    for d in (1, 2, 0):
        code = first + behind(position, d, blocks * LANES)
        for e, value in enumerate(links(seeds_here[d], code)):
            u_ref[d, e] = value
    pl.semaphore_wait(barrier, size - 1)

    def plane(k):
        return pltpu.make_async_remote_copy(
            src_ref=own_ref.at[k],
            dst_ref=near_ref.at[k],
            send_sem=plane_sems.at[0, k],
            recv_sem=plane_sems.at[1, k],
            device_id=below,
            device_id_type=MESH,
        )

    for k in range(blocks):
        for c in range(COLOURS):
            local[k * COLOURS + c].wait()
        plane(k).start()

    v = own_ref.reshape(blocks, COLOURS, 2 * modes, LANES)
    near = near_ref.reshape(blocks, COLOURS, 2 * modes, LANES)
    shift_modes(v, y_ref, z_ref)
    swap_ref[...] = jnp.zeros_like(swap_ref)
    g_ref[...] = jnp.zeros_like(g_ref)

    def swap(d):
        return pltpu.make_async_remote_copy(
            src_ref=swap_ref.at[d],
            dst_ref=got_ref.at[d],
            send_sem=swap_sems.at[0, d],
            recv_sem=swap_sems.at[1, d],
            device_id=partner,
            device_id_type=MESH,
        )

    def join(d):
        swap(d).wait()
        sum_ref[...] = (swap_ref[d].astype(F32) + got_ref[d].astype(F32)).astype(BF16)

    def gather(d, to):
        lines = jnp.dot(pick_ref[to], sum_ref[...], preferred_element_type=F32)
        part, mask = part_ref[to], mask_ref[to]
        found = []
        for r in range(TM):
            line = lines[r * rows : (r + 1) * rows]
            for t in range(2):
                at = t * modes
                x = line[:, at : at + LANES]
                for n in range(1, modes // LANES):
                    y = line[:, at + n * LANES : at + (n + 1) * LANES]
                    x = jnp.where(part == n, y, x)
                found.append((x * mask).astype(BF16))
        return jnp.dot(
            jnp.concatenate(found, 1), place_ref[d], preferred_element_type=F32
        )

    def pair_step(k, carry):
        sites = (2 * k, 2 * k + 1)
        for slot, site in enumerate(sites):
            widen(v, site, f_ref)
            fill_hops(u_ref, 1, f_ref, site, h_ref, slot)
            fill_hops(u_ref, 2, f_ref, site, h_ref, 2 + slot)
        add_products(y_ref, sites, h_ref.at[:2], g_ref.at[0])
        add_products(z_ref, sites, h_ref.at[2:], g_ref.at[1])
        return carry

    lax.fori_loop(0, blocks // 2, pair_step, 0)
    for d in (1, 2):
        derive(g_ref.at[d - 1], s_ref, swap_ref.at[d])
        swap(d).start()
    slot_copy.wait()
    prepare_slots(
        slots_here, core, flat_ref, pick_ref, mask_ref, part_ref, place_ref
    )
    for d in (1, 2):
        join(d)

        def spread_step(to, carry, d=d):
            found = gather(d, to)
            acc_ref[to] = found if d == 1 else acc_ref[to] + found
            return carry

        lax.fori_loop(0, chips, spread_step, 0)

    g_ref[0] = jnp.zeros(g_ref.shape[1:], F32)

    def near_step(k, carry):
        sites = (2 * k, 2 * k + 1)
        for slot, site in enumerate(sites):
            plane(site).wait_recv()
            widen(near, site, f_ref)
            fill_hops(u_ref, 0, f_ref, site, h_ref, slot)
        add_products(v, sites, h_ref, g_ref.at[0])
        return carry

    lax.fori_loop(0, blocks // 2 - 1, near_step, 0)

    def last_step(k, carry):
        plane(k).wait_recv()
        widen(near, k, f_ref)
        fill_hops(u_ref, 0, f_ref, k, h_ref, 0)
        add_products(v, (k,), h_ref, g_ref.at[0])
        return carry

    lax.fori_loop(blocks - 2, blocks, last_step, 0)
    derive(g_ref.at[0], s_ref, swap_ref.at[0])
    swap(0).start()
    join(0)

    def piece(step):
        to = lax.rem(chip + step, chips)
        return pltpu.make_async_remote_copy(
            src_ref=send_ref.at[to],
            dst_ref=came_ref.at[step],
            send_sem=piece_sems.at[0, step],
            recv_sem=piece_sems.at[1, step],
            device_id=(cfg, to * 2 + core),
            device_id_type=MESH,
        )

    def send_step(step, carry):
        to = lax.rem(chip + step, chips)
        send_ref[to] = (acc_ref[to] + gather(0, to)).astype(BF16)
        piece(step).start()
        return carry

    lax.fori_loop(1, chips, send_step, 0)
    total = acc_ref[chip] + gather(0, chip)
    for step in range(1, chips):
        piece(step).wait_recv()
        total = total + came_ref[step].astype(F32)
    out_ref[...] = total[:slots, :entries] * scale
    for step in range(1, chips):
        piece(step).wait_send()
    for k in range(blocks):
        plane(k).wait_send()


def per_device(eigvecs, link_seed, ownership):
    modes, _, colours, layers, sites = eigvecs.shape
    size = lax.axis_size("sx")
    chips = size // 2
    blocks = sites // LANES
    raw = (
        eigvecs.transpose(0, 2, 3, 1, 4)
        .reshape(modes, colours, 2, blocks, LANES)
        .transpose(0, 1, 3, 2, 4)
    )
    count = ownership.shape[0]
    slots = count // size
    rows = -(-slots // ROWS) * ROWS
    flat = -(-(count - slots + rows) // LANES) * LANES
    scale = 1.0 / math.sqrt(12.0 * layers * size * sites)
    vmem = pl.BlockSpec(memory_space=pltpu.VMEM)
    hbm = pl.BlockSpec(memory_space=pltpu.HBM)
    plane = pltpu.VMEM((blocks, colours, modes, 2, LANES), BF16)
    both = 2 * modes
    shifted = pltpu.VMEM((blocks, colours, both, LANES), BF16)
    derived = pltpu.VMEM((3, modes, both), BF16)
    return pl.pallas_call(
        functools.partial(main_kernel, scale),
        out_shape=jax.ShapeDtypeStruct((slots, 6 * TM * TM), F32),
        in_specs=[hbm, hbm, hbm],
        out_specs=vmem,
        scratch_shapes=[
            plane,
            plane,
            shifted,
            shifted,
            pltpu.VMEM((3, 18, blocks, LANES), F32),
            pltpu.VMEM((colours, both, LANES), F32),
            pltpu.VMEM((4, colours, both, LANES), BF16),
            pltpu.VMEM((2, both // LANES, both, LANES), F32),
            pltpu.VMEM((2, modes // LANES, modes, LANES), F32),
            derived,
            derived,
            pltpu.VMEM((modes, both), BF16),
            pltpu.VMEM((8, flat), F32),
            pltpu.VMEM((chips, TM * rows, modes), BF16),
            pltpu.VMEM((chips, rows, LANES), F32),
            pltpu.VMEM((chips, rows, LANES), jnp.int32),
            pltpu.VMEM((3, 2 * TM * LANES, LANES), BF16),
            pltpu.VMEM((chips, rows, LANES), F32),
            pltpu.VMEM((chips, rows, LANES), BF16),
            pltpu.VMEM((chips, rows, LANES), BF16),
            pltpu.VMEM((1, count), jnp.int32),
            pltpu.SMEM(link_seed.shape, jnp.int32),
            pltpu.SemaphoreType.DMA((blocks, colours)),
            pltpu.SemaphoreType.DMA((2,)),
            pltpu.SemaphoreType.DMA((2, blocks)),
            pltpu.SemaphoreType.DMA((2, 3)),
            pltpu.SemaphoreType.DMA((2, chips)),
        ],
        compiler_params=pltpu.CompilerParams(
            collective_id=0, has_side_effects=True, vmem_limit_bytes=LARGE
        ),
        name="elementals",
    )(link_seed, ownership.reshape(1, count), raw)


def solution(mesh):
    return jax.shard_map(
        per_device,
        mesh=mesh,
        in_specs=(P("cfg", None, None, "sx", None), P("cfg"), P()),
        out_specs=P(("cfg", "sx"), None),
        check_vma=False,
    )
```

time: 76.5 us -> 56.3 us (0.74)
  Pallas kernels: 72.2 us -> 53.2 us
  local copies, waits for them, and re-layouts: 3.97 us -> 2.83 us
    pallas_call x1, Pallas kernels: 72.2 us -> 53.2 us  [per_device(): pl.pallas_call(functools.partial(main_kernel, scale), out_shape=jax.Shape...]
    unnamed x5 -> x1, local copies, waits for them, and re-layouts: 3.17 us -> 1.52 us
where the time goes in v2:
time: 56.3 us; the launch traced here: 56 us
  Pallas kernels  53.2 us (94%)
  local copies, waits for them, and re-layouts  2.83 us (5%)
    pallas_call x1, Pallas kernels, per_device(): pl.pallas_call(functools.partial(main_kernel, scale), out_shape=jax.Shape...  53.2 us
    unnamed x1, local copies, waits for them, and re-layouts  1.52 us
    reshape x1, local copies, waits for them, and re-layouts, per_device(): ownership.reshape(1, count)  1.31 us

profile of v2, /device:TPU:0, one launch (start us, length us, event | category | flops | bytes accessed | tf_op | source)
XLA Modules:
  0.0 56.0 jit_solution(11715288905524116265)
XLA Ops:
  0.0 1.3 %reshape.6.slot_ref = s32[1,2080]{1,0:T(1,128)} reshape(s32[2080]{0:T(1024)} %param.5) | data formatting | bytes 16640 | tf_op jit(solution)/shard_map/reshape | solution.py:482
  1.3 53.2 %elementals.1 = f32[130,96]{1,0:T(8,128)} custom-call(s32[3]{0:T(128)} %seed_ref.1, s32[1,2080]{1,0:T(1,128)} %reshape.6.slot_ref, bf16[256,3,8,2,128]{4,3,2,1,0:T(2,128)(2,1)} %bitcast.5), custom_call_target="tpu_custom_call" | custom-call | tf_op jit(solution)/shard_map/elementals/pallas_call | solution.py:444
  54.5 1.5 %copy.5 = f32[130,96]{1,0:T(8,128)} copy(f32[130,96]{1,0:T(8,128)} %elementals.1) | data formatting | bytes 99840

commit v3 on v2

--- a/solution.py
+++ b/solution.py
@@ -14,7 +14,9 @@
 LANES = 128
 ROWS = 16
 COLOURS = 3
-LARGE = 62 * 1024 * 1024
+GROUPS = 4
+SUBLANES = 8
+LARGE = 61 * 1024 * 1024
 MESH = pl.DeviceIdType.MESH
 F32 = jnp.float32
 BF16 = jnp.bfloat16
@@ -73,31 +75,23 @@
 def shift_modes(v_ref, y_ref, z_ref):
     blocks = v_ref.shape[0]
     wide = 2 * LANES
-    row = lax.broadcasted_iota(jnp.int32, (wide, LANES), 0)
-    col = lax.broadcasted_iota(jnp.int32, (wide, LANES), 1)
-    move_y = (row == col + (LANES - NZ)).astype(F32).astype(BF16)
     row = lax.broadcasted_iota(jnp.int32, (wide, wide), 0)
     col = lax.broadcasted_iota(jnp.int32, (wide, wide), 1)
-    move_z = (row == behind(col, 2, wide)).astype(F32).astype(BF16)
+    from_y = col + (LANES - NZ)
+    from_z = LANES + behind(col - LANES, 2, wide)
+    source = jnp.where(col < LANES, from_y, from_z)
+    move = (row == source).astype(F32).astype(BF16)
 
     def step(k, carry):
         before = lax.rem(k + blocks - 1, blocks)
         for c in range(COLOURS):
             both = jnp.concatenate([v_ref[before, c], v_ref[k, c]], 1)
-            moved = jnp.dot(both, move_y, preferred_element_type=F32)
-            y_ref[k, c] = moved.astype(BF16)
+            moved = jnp.dot(both, move, preferred_element_type=F32).astype(BF16)
+            y_ref[k, c] = moved[:, :LANES]
+            z_ref[k, c] = moved[:, LANES:]
         return carry
 
-    def pair_step(k, carry):
-        for c in range(COLOURS):
-            both = jnp.concatenate([v_ref[2 * k, c], v_ref[2 * k + 1, c]], 1)
-            moved = jnp.dot(both, move_z, preferred_element_type=F32).astype(BF16)
-            z_ref[2 * k, c] = moved[:, :LANES]
-            z_ref[2 * k + 1, c] = moved[:, LANES:]
-        return carry
-
     lax.fori_loop(0, blocks, step, 0)
-    lax.fori_loop(0, blocks // 2, pair_step, 0)
 
 
 def widen(src_ref, site, f_ref):
@@ -174,38 +168,53 @@
 
 
 def prepare_slots(slot_ref, core, flat_ref, pick_ref, mask_ref, part_ref, place_ref):
-    count = slot_ref.shape[1]
+    count = slot_ref.shape[0]
     chips, rows, modes = pick_ref.shape[0], pick_ref.shape[1] // TM, pick_ref.shape[2]
     tiles = modes // TM
     slots = count // (2 * chips)
+    slot = slot_ref[...].reshape(1, count)
+
+    def start(i):
+        return i * tiles - (i * (i - 1)) // 2
+
+    edge = 2 * tiles + 1
+    root = jnp.sqrt((edge * edge - 8 * slot).astype(F32))
+    i = jnp.floor((edge - root) * 0.5).astype(jnp.int32)
+    i = jnp.where(start(i) > slot, i - 1, jnp.where(start(i + 1) <= slot, i + 1, i))
+    j = slot - start(i) + i
     flat_ref[...] = jnp.full(flat_ref.shape, -1.0, F32)
-    flat_ref[:, :count] = jnp.broadcast_to(slot_ref[...].astype(F32), (8, count))
-    column = flat_ref[...].T[:, :1]
+    flat_ref[0:1, :count] = i.astype(F32)
+    flat_ref[1:2, :count] = j.astype(F32)
+    column = flat_ref[...].T
     mode = lax.broadcasted_iota(jnp.int32, (rows, modes), 1)
-    i = mode // TM
-    start = i * tiles - (i * (i - 1)) // 2
     lane = lax.broadcasted_iota(jnp.int32, (rows, LANES), 1)
     for chip in range(chips):
         at = 2 * chip * slots
-        slot = jnp.where(
-            core == 0, column[at : at + rows], column[at + slots : at + slots + rows]
-        ).astype(jnp.int32)
-        in_row = (slot >= start) & (slot < start + tiles - i)
+        parts = []
+        for g in range(GROUPS):
+            lo = at + g * (-(-slots // GROUPS))
+            part = jnp.where(
+                core == 0,
+                column[lo : lo + rows // GROUPS, :2],
+                column[lo + slots : lo + slots + rows // GROUPS, :2],
+            )
+            parts.append(part)
+        both = jnp.concatenate(parts, 0).astype(jnp.int32)
+        i_of, j_of = both[:, :1] * TM, both[:, 1:]
         for r in range(TM):
-            pick = jnp.where(in_row & (mode % TM == r), 1.0, 0.0)
+            pick = jnp.where(mode == i_of + r, 1.0, 0.0)
             pick_ref[chip, r * rows : (r + 1) * rows] = pick.astype(BF16)
-        i_of = jnp.max(jnp.where(in_row, i, 0), axis=1, keepdims=True)
-        j_of = slot - (i_of * tiles - (i_of * (i_of - 1)) // 2) + i_of
         block = j_of // (LANES // TM)
         inside = j_of - block * (LANES // TM)
         part_ref[chip] = jnp.broadcast_to(block, (rows, LANES))
         mask_ref[chip] = jnp.where(lane // TM == inside, 1.0, 0.0)
     row = lax.broadcasted_iota(jnp.int32, (2 * TM * LANES, LANES), 0)
     col = lax.broadcasted_iota(jnp.int32, (2 * TM * LANES, LANES), 1)
-    for d in range(3):
-        r, t = row // (2 * LANES), (row // LANES) % 2
-        target = ((2 * d + t) * TM + r) * TM + row % TM
-        place_ref[d] = jnp.where(target == col, 1.0, 0.0).astype(BF16)
+    r, t = row // (2 * LANES), (row // LANES) % 2
+    target = (t * TM + r) * TM + row % TM
+    width = 2 * TM * TM
+    for n in range(place_ref.shape[0]):
+        place_ref[n] = jnp.where(target + n * width == col, 1.0, 0.0).astype(BF16)
 
 
 def main_kernel(
@@ -234,6 +243,8 @@
     acc_ref,
     send_ref,
     came_ref,
+    send_yz_ref,
+    came_yz_ref,
     slots_here,
     seeds_here,
     local_sems,
@@ -251,8 +262,8 @@
     partner = (cfg, chip * 2 + 1 - core)
     below = (cfg, lax.rem(me + size - 1, size))
     modes, _, blocks, _, _ = raw_ref.shape
-    rows = send_ref.shape[1]
-    slots, entries = out_ref.shape
+    rows = mask_ref.shape[1]
+    slots = out_ref.shape[0]
 
     barrier = pltpu.get_barrier_semaphore()
     for step in range(1, size):
@@ -319,11 +330,11 @@
 
     def join(d):
         swap(d).wait()
-        sum_ref[...] = (swap_ref[d].astype(F32) + got_ref[d].astype(F32)).astype(BF16)
-
-    def gather(d, to):
-        lines = jnp.dot(pick_ref[to], sum_ref[...], preferred_element_type=F32)
+        sum_ref[d] = (swap_ref[d].astype(F32) + got_ref[d].astype(F32)).astype(BF16)
+
+    def pick(d, to):
         part, mask = part_ref[to], mask_ref[to]
+        lines = jnp.dot(pick_ref[to], sum_ref[d], preferred_element_type=F32)
         found = []
         for r in range(TM):
             line = lines[r * rows : (r + 1) * rows]
@@ -334,9 +345,62 @@
                     y = line[:, at + n * LANES : at + (n + 1) * LANES]
                     x = jnp.where(part == n, y, x)
                 found.append((x * mask).astype(BF16))
-        return jnp.dot(
-            jnp.concatenate(found, 1), place_ref[d], preferred_element_type=F32
+        return jnp.concatenate(found, 1)
+
+    def gather(ds, to):
+        found = jnp.concatenate([pick(d, to) for d in ds], 1)
+        place = jnp.concatenate([place_ref[m] for m in range(len(ds))], 0)
+        lines = jnp.dot(found, place, preferred_element_type=F32)
+        sets = GROUPS // len(ds)
+        each = rows // sets
+        total = lines[:each]
+        for n in range(1, sets):
+            line = lines[n * each : (n + 1) * each]
+            total = total + pltpu.roll(line, n * (LANES // sets), 1)
+        return total
+
+    def target(n):
+        upper = (2 * chip) // chips
+        rising = n + (n - chip + chips) // chips
+        falling = chips - 1 - n
+        falling = falling - (chip - falling + chips) // chips
+        return upper * rising + (1 - upper) * falling
+
+    def piece(kind, to, origin):
+        send, came = ((send_ref, came_ref), (send_yz_ref, came_yz_ref))[kind]
+        return pltpu.make_async_remote_copy(
+            src_ref=send.at[to],
+            dst_ref=came.at[origin],
+            send_sem=piece_sems.at[2 * kind, to],
+            recv_sem=piece_sems.at[2 * kind + 1, origin],
+            device_id=(cfg, to * 2 + core),
+            device_id_type=MESH,
         )
+
+    def post(kind, ds):
+        send = (send_ref, send_yz_ref)[kind]
+
+        def post_step(n, carry):
+            to = target(n)
+            send[to] = gather(ds, to).astype(BF16)
+            if kind == 0:
+                piece(kind, to, chip).start()
+            return carry
+
+        lax.fori_loop(0, chips - 1, post_step, 0)
+        return gather(ds, chip)
+
+    def collect(kind, total):
+        came = (came_ref, came_yz_ref)[kind]
+        for step in range(1, chips):
+            origin = lax.rem(chip + step, chips)
+            piece(kind, origin, origin).wait_recv()
+            total = total + came[origin].astype(F32)
+        return total * scale
+
+    def sent(kind):
+        for step in range(1, chips):
+            piece(kind, lax.rem(chip + step, chips), chip).wait_send()
 
     def pair_step(k, carry):
         sites = (2 * k, 2 * k + 1)
@@ -359,13 +423,7 @@
     for d in (1, 2):
         join(d)
 
-        def spread_step(to, carry, d=d):
-            found = gather(d, to)
-            acc_ref[to] = found if d == 1 else acc_ref[to] + found
-            return carry
-
-        lax.fori_loop(0, chips, spread_step, 0)
-
+    acc_ref[...] = post(1, (1, 2))
     g_ref[0] = jnp.zeros(g_ref.shape[1:], F32)
 
     def near_step(k, carry):
@@ -379,44 +437,42 @@
 
     lax.fori_loop(0, blocks // 2 - 1, near_step, 0)
 
-    def last_step(k, carry):
-        plane(k).wait_recv()
+    def use_plane(k):
         widen(near, k, f_ref)
         fill_hops(u_ref, 0, f_ref, k, h_ref, 0)
         add_products(v, (k,), h_ref, g_ref.at[0])
+
+    plane(blocks - 2).wait_recv()
+    use_plane(blocks - 2)
+    plane(blocks - 1).wait_send()
+    plane(blocks - 1).wait_recv()
+
+    def launch_step(n, carry):
+        piece(1, target(n), chip).start()
         return carry
 
-    lax.fori_loop(blocks - 2, blocks, last_step, 0)
+    lax.fori_loop(0, chips - 1, launch_step, 0)
+    use_plane(blocks - 1)
     derive(g_ref.at[0], s_ref, swap_ref.at[0])
     swap(0).start()
     join(0)
 
-    def piece(step):
-        to = lax.rem(chip + step, chips)
-        return pltpu.make_async_remote_copy(
-            src_ref=send_ref.at[to],
-            dst_ref=came_ref.at[step],
-            send_sem=piece_sems.at[0, step],
-            recv_sem=piece_sems.at[1, step],
-            device_id=(cfg, to * 2 + core),
-            device_id_type=MESH,
-        )
-
-    def send_step(step, carry):
-        to = lax.rem(chip + step, chips)
-        send_ref[to] = (acc_ref[to] + gather(0, to)).astype(BF16)
-        piece(step).start()
-        return carry
-
-    lax.fori_loop(1, chips, send_step, 0)
-    total = acc_ref[chip] + gather(0, chip)
-    for step in range(1, chips):
-        piece(step).wait_recv()
-        total = total + came_ref[step].astype(F32)
-    out_ref[...] = total[:slots, :entries] * scale
-    for step in range(1, chips):
-        piece(step).wait_send()
-    for k in range(blocks):
+    here = post(0, (0,))
+    acc_ref[...] = collect(1, acc_ref[...])
+    total = collect(0, here)
+    per = -(-slots // GROUPS)
+    each = rows // GROUPS
+    width = 2 * TM * TM
+    for g in range(GROUPS):
+        take = min(per, slots - g * per)
+        first_rows = slice((g % 2) * each, (g % 2) * each + take)
+        lanes = slice((g // 2) * 2 * width, (g // 2 + 1) * 2 * width)
+        at = slice(g * per, g * per + take)
+        out_ref[at, :width] = total[:take, g * width : (g + 1) * width]
+        out_ref[at, width:] = acc_ref[first_rows, lanes]
+    sent(0)
+    sent(1)
+    for k in range(blocks - 1):
         plane(k).wait_send()
 
 
@@ -432,8 +488,10 @@
     )
     count = ownership.shape[0]
     slots = count // size
-    rows = -(-slots // ROWS) * ROWS
-    flat = -(-(count - slots + rows) // LANES) * LANES
+    per = -(-slots // GROUPS)
+    each = -(-per // SUBLANES) * SUBLANES
+    rows = GROUPS * each
+    flat = -(-(count - slots + (GROUPS - 1) * per + each) // LANES) * LANES
     scale = 1.0 / math.sqrt(12.0 * layers * size * sites)
     vmem = pl.BlockSpec(memory_space=pltpu.VMEM)
     hbm = pl.BlockSpec(memory_space=pltpu.HBM)
@@ -458,28 +516,30 @@
             pltpu.VMEM((2, modes // LANES, modes, LANES), F32),
             derived,
             derived,
-            pltpu.VMEM((modes, both), BF16),
+            derived,
             pltpu.VMEM((8, flat), F32),
             pltpu.VMEM((chips, TM * rows, modes), BF16),
             pltpu.VMEM((chips, rows, LANES), F32),
             pltpu.VMEM((chips, rows, LANES), jnp.int32),
-            pltpu.VMEM((3, 2 * TM * LANES, LANES), BF16),
-            pltpu.VMEM((chips, rows, LANES), F32),
-            pltpu.VMEM((chips, rows, LANES), BF16),
-            pltpu.VMEM((chips, rows, LANES), BF16),
-            pltpu.VMEM((1, count), jnp.int32),
+            pltpu.VMEM((2, 2 * TM * LANES, LANES), BF16),
+            pltpu.VMEM((2 * each, LANES), F32),
+            pltpu.VMEM((chips, each, LANES), BF16),
+            pltpu.VMEM((chips, each, LANES), BF16),
+            pltpu.VMEM((chips, 2 * each, LANES), BF16),
+            pltpu.VMEM((chips, 2 * each, LANES), BF16),
+            pltpu.VMEM((count,), jnp.int32),
             pltpu.SMEM(link_seed.shape, jnp.int32),
             pltpu.SemaphoreType.DMA((blocks, colours)),
             pltpu.SemaphoreType.DMA((2,)),
             pltpu.SemaphoreType.DMA((2, blocks)),
             pltpu.SemaphoreType.DMA((2, 3)),
-            pltpu.SemaphoreType.DMA((2, chips)),
+            pltpu.SemaphoreType.DMA((4, chips)),
         ],
         compiler_params=pltpu.CompilerParams(
             collective_id=0, has_side_effects=True, vmem_limit_bytes=LARGE
         ),
         name="elementals",
-    )(link_seed, ownership.reshape(1, count), raw)
+    )(link_seed, ownership, raw)
 
 
 def solution(mesh):

time: 56.3 us -> 54 us (0.959)
  local copies, waits for them, and re-layouts: 2.83 us -> 1.52 us
  Pallas kernels: 53.2 us -> 52.3 us
    reshape x1 -> x0, local copies, waits for them, and re-layouts: 1.31 us -> none  [per_device(): ownership.reshape(1, count)]
    pallas_call x1, Pallas kernels: 53.2 us -> 52.3 us  [per_device(): pl.pallas_call(functools.partial(main_kernel, scale), out_shape=jax.Shape...]
where the time goes in v3:
time: 54 us; the launch traced here: 53.9 us
  Pallas kernels  52.3 us (97%)
  local copies, waits for them, and re-layouts  1.52 us (3%)
    pallas_call x1, Pallas kernels, per_device(): pl.pallas_call(functools.partial(main_kernel, scale), out_shape=jax.Shape...  52.3 us
    unnamed x1, local copies, waits for them, and re-layouts  1.52 us

profile of v3, /device:TPU:0, one launch (start us, length us, event | category | flops | bytes accessed | tf_op | source)
XLA Modules:
  0.0 53.9 jit_solution(2827294138098513466)
XLA Ops:
  0.0 52.3 %elementals.1 = f32[130,96]{1,0:T(8,128)} custom-call(s32[3]{0:T(128)} %seed_ref.1, s32[2080]{0:T(1024)} %slot_ref.1, bf16[256,3,8,2,128]{4,3,2,1,0:T(2,128)(2,1)} %bitcast.5), custom_call_target="tpu_custom_call" | custom-call | tf_op jit(solution)/shard_map/elementals/pallas_call | solution.py:502
  52.3 1.5 %copy.5 = f32[130,96]{1,0:T(8,128)} copy(f32[130,96]{1,0:T(8,128)} %elementals.1) | data formatting | bytes 99840

commit v4 on v3

--- a/solution.py
+++ b/solution.py
@@ -16,7 +16,7 @@
 COLOURS = 3
 GROUPS = 4
 SUBLANES = 8
-LARGE = 61 * 1024 * 1024
+LARGE = 52 * 1024 * 1024
 MESH = pl.DeviceIdType.MESH
 F32 = jnp.float32
 BF16 = jnp.bfloat16
@@ -94,13 +94,15 @@
     lax.fori_loop(0, blocks, step, 0)
 
 
-def widen(src_ref, site, f_ref):
+def widen(src_ref, site, f_ref, lo=0, hi=None):
+    rows = slice(2 * lo, f_ref.shape[1] if hi is None else 2 * hi)
     for c in range(COLOURS):
-        f_ref[c] = src_ref[site, c].astype(F32)
-
-
-def fill_hops(u_ref, d, f_ref, site, h_ref, slot):
+        f_ref[c, rows] = src_ref[site, c, rows].astype(F32)
+
+
+def fill_hops(u_ref, d, f_ref, site, h_ref, slot, lo=0, hi=None):
     modes = f_ref.shape[1] // 2
+    hi = modes if hi is None else hi
 
     def entry(e):
         return jnp.broadcast_to(u_ref[d, e, pl.ds(site, 1), :], (8, LANES))
@@ -131,7 +133,7 @@
             h_ref[slot, q % 3, pl.ds(at, ROWS)] = both
         return carry
 
-    lax.fori_loop(0, modes // ROWS, rows_step, 0, unroll=2)
+    lax.fori_loop(lo // ROWS, hi // ROWS, rows_step, 0, unroll=2)
 
 
 def add_products(w_ref, sites, h_ref, g_ref):
@@ -146,25 +148,37 @@
         g_ref[n] += term[:, n * LANES : (n + 1) * LANES]
 
 
-def derive(g_ref, s_ref, e_ref):
+def add_block(w_ref, site, h_ref, g_ref, n):
+    modes = h_ref.shape[2] // 2
+    left = jnp.concatenate([w_ref[site, c] for c in range(COLOURS)], 1)
+    rows = [slice(t * modes + n * LANES, t * modes + (n + 1) * LANES) for t in range(2)]
+    right = jnp.concatenate(
+        [
+            jnp.concatenate([h_ref[0, c, at] for c in range(COLOURS)], 1)
+            for at in rows
+        ],
+        0,
+    )
+    term = lax.dot_general(left, right, NT, preferred_element_type=F32)
+    g_ref[n] += term[:, :LANES]
+    g_ref[modes // LANES + n] += term[:, LANES:]
+
+
+def derive(g_ref, s_ref, e_ref, t):
     parts, both, _ = g_ref.shape
     modes = both // 2
     count = parts // 2
     for n in range(count):
-        here = [g_ref[n, pl.ds(t, modes, stride=2), :] for t in range(2)]
-        there = [g_ref[count + n, pl.ds(t, modes, stride=2), :] for t in range(2)]
-        s_ref[0, n] = here[0] + there[1]
-        s_ref[1, n] = there[0] - here[1]
+        here = g_ref[n, pl.ds(t, modes, stride=2), :]
+        there = g_ref[count + n, pl.ds(1 - t, modes, stride=2), :]
+        s_ref[n] = here + there if t == 0 else there - here
     for j in range(count):
         for i in range(j + 1):
             rows, cols = slice(i * LANES, (i + 1) * LANES), slice(j * LANES, (j + 1) * LANES)
-            at = j * LANES
-            e_ref[rows, at : at + LANES] = (
-                s_ref[0, j, rows] - s_ref[0, i, cols].T
-            ).astype(BF16)
-            e_ref[rows, modes + at : modes + at + LANES] = (
-                s_ref[1, j, rows] + s_ref[1, i, cols].T
-            ).astype(BF16)
+            mirror = s_ref[i, cols].T
+            value = s_ref[j, rows] - mirror if t == 0 else s_ref[j, rows] + mirror
+            at = t * modes + j * LANES
+            e_ref[rows, at : at + LANES] = value.astype(BF16)
 
 
 def prepare_slots(slot_ref, core, flat_ref, pick_ref, mask_ref, part_ref, place_ref):
@@ -250,6 +264,7 @@
     local_sems,
     small_sems,
     plane_sems,
+    tail_sems,
     swap_sems,
     piece_sems,
 ):
@@ -297,6 +312,17 @@
             u_ref[d, e] = value
     pl.semaphore_wait(barrier, size - 1)
 
+    def tail(n):
+        k, part = blocks - 1, pl.ds(n * LANES, LANES)
+        return pltpu.make_async_remote_copy(
+            src_ref=own_ref.at[k, :, part],
+            dst_ref=near_ref.at[k, :, part],
+            send_sem=tail_sems.at[0, n],
+            recv_sem=tail_sems.at[1, n],
+            device_id=below,
+            device_id_type=MESH,
+        )
+
     def plane(k):
         return pltpu.make_async_remote_copy(
             src_ref=own_ref.at[k],
@@ -310,7 +336,10 @@
     for k in range(blocks):
         for c in range(COLOURS):
             local[k * COLOURS + c].wait()
-        plane(k).start()
+        if k < blocks - 1:
+            plane(k).start()
+    for n in range(modes // LANES):
+        tail(n).start()
 
     v = own_ref.reshape(blocks, COLOURS, 2 * modes, LANES)
     near = near_ref.reshape(blocks, COLOURS, 2 * modes, LANES)
@@ -318,19 +347,28 @@
     swap_ref[...] = jnp.zeros_like(swap_ref)
     g_ref[...] = jnp.zeros_like(g_ref)
 
-    def swap(d):
+    def swap(d, t):
+        lanes = pl.ds(t * modes, modes)
         return pltpu.make_async_remote_copy(
-            src_ref=swap_ref.at[d],
-            dst_ref=got_ref.at[d],
-            send_sem=swap_sems.at[0, d],
-            recv_sem=swap_sems.at[1, d],
+            src_ref=swap_ref.at[d, :, lanes],
+            dst_ref=got_ref.at[d, :, lanes],
+            send_sem=swap_sems.at[t, d],
+            recv_sem=swap_sems.at[2 + t, d],
             device_id=partner,
             device_id_type=MESH,
         )
 
+    def finish(d, products_ref):
+        for t in range(2):
+            derive(products_ref, s_ref, swap_ref.at[d], t)
+            swap(d, t).start()
+
     def join(d):
-        swap(d).wait()
-        sum_ref[d] = (swap_ref[d].astype(F32) + got_ref[d].astype(F32)).astype(BF16)
+        for t in range(2):
+            lanes = slice(t * modes, (t + 1) * modes)
+            swap(d, t).wait_recv()
+            total = swap_ref[d, :, lanes].astype(F32) + got_ref[d, :, lanes].astype(F32)
+            sum_ref[d, :, lanes] = total.astype(BF16)
 
     def pick(d, to):
         part, mask = part_ref[to], mask_ref[to]
@@ -414,8 +452,7 @@
 
     lax.fori_loop(0, blocks // 2, pair_step, 0)
     for d in (1, 2):
-        derive(g_ref.at[d - 1], s_ref, swap_ref.at[d])
-        swap(d).start()
+        finish(d, g_ref.at[d - 1])
     slot_copy.wait()
     prepare_slots(
         slots_here, core, flat_ref, pick_ref, mask_ref, part_ref, place_ref
@@ -437,6 +474,12 @@
 
     lax.fori_loop(0, blocks // 2 - 1, near_step, 0)
 
+    def use_part(n):
+        lo, hi = n * LANES, (n + 1) * LANES
+        widen(near, blocks - 1, f_ref, lo, hi)
+        fill_hops(u_ref, 0, f_ref, blocks - 1, h_ref, 0, lo, hi)
+        add_block(v, blocks - 1, h_ref, g_ref.at[0], n)
+
     def use_plane(k):
         widen(near, k, f_ref)
         fill_hops(u_ref, 0, f_ref, k, h_ref, 0)
@@ -444,34 +487,44 @@
 
     plane(blocks - 2).wait_recv()
     use_plane(blocks - 2)
-    plane(blocks - 1).wait_send()
-    plane(blocks - 1).wait_recv()
-
-    def launch_step(n, carry):
-        piece(1, target(n), chip).start()
-        return carry
-
-    lax.fori_loop(0, chips - 1, launch_step, 0)
-    use_plane(blocks - 1)
-    derive(g_ref.at[0], s_ref, swap_ref.at[0])
-    swap(0).start()
+    def launch():
+        def launch_step(n, carry):
+            piece(1, target(n), chip).start()
+            return carry
+
+        lax.fori_loop(0, chips - 1, launch_step, 0)
+
+    for n in range(modes // LANES):
+        tail(n).wait_recv()
+        if n == modes // LANES - 1:
+            pl.when(core == 1)(launch)
+        use_part(n)
+    finish(0, g_ref.at[0])
+    for n in range(modes // LANES):
+        tail(n).wait_send()
+    pl.when(core == 0)(launch)
     join(0)
 
     here = post(0, (0,))
-    acc_ref[...] = collect(1, acc_ref[...])
-    total = collect(0, here)
     per = -(-slots // GROUPS)
     each = rows // GROUPS
     width = 2 * TM * TM
-    for g in range(GROUPS):
-        take = min(per, slots - g * per)
-        first_rows = slice((g % 2) * each, (g % 2) * each + take)
-        lanes = slice((g // 2) * 2 * width, (g // 2 + 1) * 2 * width)
-        at = slice(g * per, g * per + take)
-        out_ref[at, :width] = total[:take, g * width : (g + 1) * width]
-        out_ref[at, width:] = acc_ref[first_rows, lanes]
+
+    def place_out(value, sets, columns):
+        lanes = LANES // sets
+        for g in range(GROUPS):
+            take = min(per, slots - g * per)
+            n, m = divmod(g, GROUPS // sets)
+            part = value[m * each : m * each + take, n * lanes : (n + 1) * lanes]
+            out_ref[g * per : g * per + take, columns] = part
+
+    place_out(collect(1, acc_ref[...]), 2, slice(width, 3 * width))
+    place_out(collect(0, here), 4, slice(0, width))
     sent(0)
     sent(1)
+    for d in range(3):
+        for t in range(2):
+            swap(d, t).wait_send()
     for k in range(blocks - 1):
         plane(k).wait_send()
 
@@ -513,7 +566,7 @@
             pltpu.VMEM((colours, both, LANES), F32),
             pltpu.VMEM((4, colours, both, LANES), BF16),
             pltpu.VMEM((2, both // LANES, both, LANES), F32),
-            pltpu.VMEM((2, modes // LANES, modes, LANES), F32),
+            pltpu.VMEM((modes // LANES, modes, LANES), F32),
             derived,
             derived,
             derived,
@@ -532,14 +585,15 @@
             pltpu.SemaphoreType.DMA((blocks, colours)),
             pltpu.SemaphoreType.DMA((2,)),
             pltpu.SemaphoreType.DMA((2, blocks)),
-            pltpu.SemaphoreType.DMA((2, 3)),
+            pltpu.SemaphoreType.DMA((2, modes // LANES)),
+            pltpu.SemaphoreType.DMA((4, 3)),
             pltpu.SemaphoreType.DMA((4, chips)),
         ],
         compiler_params=pltpu.CompilerParams(
             collective_id=0, has_side_effects=True, vmem_limit_bytes=LARGE
         ),
         name="elementals",
-    )(link_seed, ownership, raw)
+    )(*[pltpu.with_memory_space_constraint(x, pltpu.HBM) for x in (link_seed, ownership, raw)])
 
 
 def solution(mesh):

time: 54 us -> 52.2 us (0.967)
  Pallas kernels: 52.3 us -> 51.4 us
  local copies, waits for them, and re-layouts: 1.52 us -> 0.63 us
    pallas_call x1, Pallas kernels: 52.3 us -> 51.4 us  [per_device(): pl.pallas_call(functools.partial(main_kernel, scale), out_shape=jax.Shape...]
    unnamed x1, local copies, waits for them, and re-layouts: 1.52 us -> 0.63 us
where the time goes in v4:
time: 52.2 us; the launch traced here: 52 us
  Pallas kernels  51.4 us (98%)
  local copies, waits for them, and re-layouts  0.63 us (1%)
    pallas_call x1, Pallas kernels, per_device(): pl.pallas_call(functools.partial(main_kernel, scale), out_shape=jax.Shape...  51.4 us

profile of v4, /device:TPU:0, one launch (start us, length us, event | category | flops | bytes accessed | tf_op | source)
XLA Modules:
  0.0 52.0 jit_solution(3302954561718136019)
XLA Ops:
  0.0 51.4 %elementals.1 = f32[130,96]{1,0:T(8,128)S(1)} custom-call(s32[3]{0:T(128)} %seed_ref.1, s32[2080]{0:T(1024)} %slot_ref.1, bf16[256,3,8,2,128]{4,3,2,1,0:T(2,128)(2,1)} %bitcast.5), custom_call_target="tpu_custom_call" | custom-call | tf_op jit(solution)/shard_map/elementals/pallas_call | solution.py:555
  51.4 0.6 %copy.5 = f32[130,96]{1,0:T(8,128)} copy(f32[130,96]{1,0:T(8,128)S(1)} %elementals.1) | data formatting | bytes 99840

commit v5 on v4

--- a/solution.py
+++ b/solution.py
@@ -301,15 +301,6 @@
             local[-1].start()
     slot_copy = pltpu.make_async_copy(slot_ref, slots_here, small_sems.at[1])
     slot_copy.start()
-    first = me * (blocks * LANES)
-    position = lax.broadcasted_iota(
-        jnp.int32, (blocks, LANES), 0
-    ) * LANES + lax.broadcasted_iota(jnp.int32, (blocks, LANES), 1)
-    seed_copy.wait()
-    for d in (1, 2, 0):
-        code = first + behind(position, d, blocks * LANES)
-        for e, value in enumerate(links(seeds_here[d], code)):
-            u_ref[d, e] = value
     pl.semaphore_wait(barrier, size - 1)
 
     def tail(n):
@@ -340,6 +331,16 @@
             plane(k).start()
     for n in range(modes // LANES):
         tail(n).start()
+
+    first = me * (blocks * LANES)
+    position = lax.broadcasted_iota(
+        jnp.int32, (blocks, LANES), 0
+    ) * LANES + lax.broadcasted_iota(jnp.int32, (blocks, LANES), 1)
+    seed_copy.wait()
+    for d in (1, 2, 0):
+        code = first + behind(position, d, blocks * LANES)
+        for e, value in enumerate(links(seeds_here[d], code)):
+            u_ref[d, e] = value
 
     v = own_ref.reshape(blocks, COLOURS, 2 * modes, LANES)
     near = near_ref.reshape(blocks, COLOURS, 2 * modes, LANES)
@@ -496,13 +497,11 @@
 
     for n in range(modes // LANES):
         tail(n).wait_recv()
-        if n == modes // LANES - 1:
-            pl.when(core == 1)(launch)
         use_part(n)
     finish(0, g_ref.at[0])
     for n in range(modes // LANES):
         tail(n).wait_send()
-    pl.when(core == 0)(launch)
+    launch()
     join(0)
 
     here = post(0, (0,))

time: 52.2 us -> 52.2 us (level)
  no operation moved by 1% of the time
where the time goes in v5:
time: 52.2 us; the launch traced here: 52 us
  Pallas kernels  51.4 us (98%)
  local copies, waits for them, and re-layouts  0.63 us (1%)
    pallas_call x1, Pallas kernels, per_device(): pl.pallas_call(functools.partial(main_kernel, scale), out_shape=jax.Shape...  51.4 us

profile of v5, /device:TPU:0, one launch (start us, length us, event | category | flops | bytes accessed | tf_op | source)
XLA Modules:
  0.0 52.0 jit_solution(5214380275922189988)
XLA Ops:
  0.0 51.4 %elementals.1 = f32[130,96]{1,0:T(8,128)S(1)} custom-call(s32[3]{0:T(128)} %seed_ref.1, s32[2080]{0:T(1024)} %slot_ref.1, bf16[256,3,8,2,128]{4,3,2,1,0:T(2,128)(2,1)} %bitcast.5), custom_call_target="tpu_custom_call" | custom-call | tf_op jit(solution)/shard_map/elementals/pallas_call | solution.py:554
  51.4 0.6 %copy.5 = f32[130,96]{1,0:T(8,128)} copy(f32[130,96]{1,0:T(8,128)S(1)} %elementals.1) | data formatting | bytes 99840

commit v6 on v5

--- a/solution.py
+++ b/solution.py
@@ -133,7 +133,7 @@
             h_ref[slot, q % 3, pl.ds(at, ROWS)] = both
         return carry
 
-    lax.fori_loop(lo // ROWS, hi // ROWS, rows_step, 0, unroll=2)
+    lax.fori_loop(lo // ROWS, hi // ROWS, rows_step, 0, unroll=4)
 
 
 def add_products(w_ref, sites, h_ref, g_ref):

time: 52.2 us -> 52.2 us (level)
  no operation moved by 1% of the time
where the time goes in v6:
time: 52.2 us; the launch traced here: 52 us
  Pallas kernels  51.4 us (98%)
  local copies, waits for them, and re-layouts  0.63 us (1%)
    pallas_call x1, Pallas kernels, per_device(): pl.pallas_call(functools.partial(main_kernel, scale), out_shape=jax.Shape...  51.4 us

profile of v6, /device:TPU:0, one launch (start us, length us, event | category | flops | bytes accessed | tf_op | source)
XLA Modules:
  0.0 52.0 jit_solution(9363233147792451642)
XLA Ops:
  0.0 51.4 %elementals.1 = f32[130,96]{1,0:T(8,128)S(1)} custom-call(s32[3]{0:T(128)} %seed_ref.1, s32[2080]{0:T(1024)} %slot_ref.1, bf16[256,3,8,2,128]{4,3,2,1,0:T(2,128)(2,1)} %bitcast.5), custom_call_target="tpu_custom_call" | custom-call | tf_op jit(solution)/shard_map/elementals/pallas_call | solution.py:554
  51.4 0.6 %copy.5 = f32[130,96]{1,0:T(8,128)} copy(f32[130,96]{1,0:T(8,128)S(1)} %elementals.1) | data formatting | bytes 99840
